TPU v7x, 512 devices: a whole 4x4x16 slice. The times are simulated.
512 devices in a mesh: seq: 64 (over z_lo, y, core), tp: 8 (over z_hi, x).
Axes of the slice: x: 4, y: 4, z: 16 (z_hi: 2, z_lo: 8; z = z_hi * 8 + z_lo), core: 2. Of those that a mesh axis runs over, the one named last changes fastest.
Arguments:
- queries: bfloat16 [16384, 2048], P('seq', 'tp'), may hold values from -42 to 42
- keys: bfloat16 [16384, 2048], P('seq', 'tp'), may hold values from -6.1 to 6.1
- values: bfloat16 [16384, 2048], P('seq', 'tp'), may hold values from -6 to 6
- residual_in: bfloat16 [16384, 2048], P('seq', 'tp'), may hold values from -6 to 6
- bias_table: float32 [16, 32], P('tp'), may hold values from -4 to 4
- buckets: int32 [128, 33], P('seq'), may hold values from 0 to 31
- out_weight: bfloat16 [2048, 2048], P('tp'), may hold values from -0.125 to 0.125
- gate_weight: bfloat16 [2048, 4096], P('seq', 'tp'), may hold values from -0.125 to 0.125
- up_weight: bfloat16 [2048, 4096], P('seq', 'tp'), may hold values from -0.125 to 0.125
- down_weight_t: bfloat16 [2048, 4096], P('seq', 'tp'), may hold values from -0.09375 to 0.09375
- norm_gain: float32 [2048], replicated, may hold values from 0.5 to 1.5
Outputs:
- layer_out: bfloat16 [16384, 2048], P('seq', 'tp')
All inputs are finite; a program needn't handle non-finite values.
Results may differ from a plain program's by a relative error of at most 0.015.
Values may be sent and summed in bfloat16 or wider, within the bound.
A program may use at most 64 MiB of HBM per device.

v0:
```python
import jax
import jax.numpy as jnp
from jax import lax
from jax.sharding import PartitionSpec as P

HEAD_DIM = 128
BUCKETS = 32
TILE = 128
HALF_BAND = 2048
OFFSETS = 33


def shifted(x, axis, by):
    devices = lax.axis_size(axis)
    pairs = [(i, i + by) for i in range(devices) if 0 <= i + by < devices]
    return lax.ppermute(x, axis, pairs)


def attend_local(queries, extended, bucket_blk, table, start, total_len, width):
    rows = queries.shape[0]
    heads = table.shape[0]
    span = rows + 2 * width
    q3 = queries.reshape(rows, heads, HEAD_DIM)
    k3 = extended[0].reshape(span, heads, HEAD_DIM)
    v3 = extended[1].reshape(span, heads, HEAD_DIM)
    scores = jnp.einsum("qhd,khd->hqk", q3, k3, preferred_element_type=jnp.float32) * HEAD_DIM ** (
        -0.5
    )
    tiles_q = rows // TILE
    tiles_k = span // TILE
    onehot = (bucket_blk[:, :, None] == jnp.arange(BUCKETS, dtype=jnp.int32)[None, None, :]).astype(
        jnp.float32
    )
    table_vals = jnp.einsum("qob,hb->hqo", onehot, table, precision=lax.Precision.HIGHEST)
    offset = (
        jnp.arange(tiles_k, dtype=jnp.int32)[None, :]
        - jnp.arange(tiles_q, dtype=jnp.int32)[:, None]
    )
    select = (offset[:, :, None] == jnp.arange(OFFSETS, dtype=jnp.int32)[None, None, :]).astype(
        jnp.float32
    )
    tile_bias = jnp.einsum("qko,hqo->hqk", select, table_vals, precision=lax.Precision.HIGHEST)
    scores = scores.reshape(heads, tiles_q, TILE, tiles_k, TILE) + tile_bias[:, :, None, :, None]
    scores = scores.reshape(heads, rows, span)
    qpos = start + jnp.arange(rows, dtype=jnp.int32)[:, None]
    kpos = start - width + jnp.arange(span, dtype=jnp.int32)[None, :]
    valid = (jnp.abs(qpos - kpos) <= width) & (kpos >= 0) & (kpos < total_len)
    masked = jnp.where(valid[None], scores, -1e30)
    top = jnp.max(masked, axis=-1, keepdims=True)
    expo = jnp.where(valid[None], jnp.exp(masked - top), 0.0)
    weight = (expo / jnp.sum(expo, axis=-1, keepdims=True)).astype(jnp.bfloat16)
    out = jnp.einsum("hqk,khd->qhd", weight, v3, preferred_element_type=jnp.float32)
    return out.astype(jnp.bfloat16).reshape(rows, heads * HEAD_DIM)


def normalize(full_state, norm_gain):
    wide = full_state.astype(jnp.float32)
    scale = lax.rsqrt(jnp.mean(wide * wide, axis=-1, keepdims=True) + 1e-05)
    return (wide * scale * norm_gain).astype(jnp.bfloat16)


def shards(
    queries,
    keys,
    values,
    residual_in,
    bias_table,
    buckets,
    out_weight,
    gate_weight,
    up_weight,
    down_weight_t,
    norm_gain,
):
    rows = queries.shape[0]
    width = HALF_BAND
    reach = width // rows
    paired = jnp.stack([keys, values], 0)
    offsets_list = list(range(reach, 0, -1)) + list(range(-1, -reach - 1, -1))
    arrived = []
    for distance in offsets_list:
        arrived.append(shifted(paired, "seq", distance))
    extended = jnp.concatenate(arrived[:reach] + [paired] + arrived[reach:], axis=1)
    start = lax.axis_index("seq") * rows
    total_len = rows * lax.axis_size("seq")
    attended = attend_local(queries, extended, buckets, bias_table, start, total_len, width)
    partial_value = jnp.dot(attended, out_weight, preferred_element_type=jnp.float32)
    own_sum = lax.psum_scatter(
        partial_value.astype(jnp.bfloat16), "tp", scatter_dimension=1, tiled=True
    ).astype(jnp.float32)
    own_state = (residual_in.astype(jnp.float32) + own_sum).astype(jnp.bfloat16)
    full_state = lax.all_gather(own_state, "tp", axis=1, tiled=True)
    normed = normalize(full_state, norm_gain)
    gate_all, up_all, down_all = (
        lax.all_gather(gate_weight, "seq", axis=0, tiled=True),
        lax.all_gather(up_weight, "seq", axis=0, tiled=True),
        lax.all_gather(down_weight_t, "seq", axis=0, tiled=True),
    )
    gate = jnp.dot(normed, gate_all, preferred_element_type=jnp.float32)
    up = jnp.dot(normed, up_all, preferred_element_type=jnp.float32)
    hidden = (jax.nn.silu(gate) * up).astype(jnp.bfloat16)
    terms = lax.dot_general(
        hidden, down_all, (((1,), (1,)), ((), ())), preferred_element_type=jnp.float32
    )
    ffn_own = lax.psum_scatter(
        terms.astype(jnp.bfloat16), "tp", scatter_dimension=1, tiled=True
    ).astype(jnp.float32)
    return (own_state.astype(jnp.float32) + ffn_own).astype(jnp.bfloat16)


def solution(mesh):
    return jax.shard_map(
        shards,
        mesh=mesh,
        in_specs=(
            P("seq", "tp"),
            P("seq", "tp"),
            P("seq", "tp"),
            P("seq", "tp"),
            P("tp", None),
            P("seq", None),
            P("tp", None),
            P("seq", "tp"),
            P("seq", "tp"),
            P("seq", "tp"),
            P(),
        ),
        out_specs=P("seq", "tp"),
        check_vma=False,
    )
```

profile of v0, /device:TPU:1, one launch (start us, length us, event | category | flops | bytes accessed | tf_op | source)
XLA Modules:
  0.0 815.4 jit_solution(12422391377847241001)
XLA Ops:
  8.7 5.1 collective-permute-start
  13.8 4.4 collective-permute-start.1
  18.2 3.9 collective-permute-start.2
  22.1 3.3 collective-permute-start.3
  25.5 4.5 collective-permute-start.4
  30.9 3.7 fusion.4
  35.0 5.9 add.69
  40.9 12.3 %add.70 = f32[2,256,4352]{1,2,0:T(8,128)} reshape(f32[2,2,128,34,128]{2,1,4,3,0:T(2,128)} %add.69) | data formatting | bytes 17825792 | tf_op jit(solution)/shard_map/add | solution.py:43
  53.2 5.7 collective-permute-start.5
  59.8 2.6 collective-permute-start.6
  63.4 2.5 collective-permute-start.7
  66.0 1.9 collective-permute-start.8
  76.2 2.2 collective-permute-done.9
  82.3 1.9 collective-permute-done.11
  84.3 6.4 collective-permute-done.12
  90.9 26.0 %collective-permute-done.14 = bf16[2,256,256]{1,2,0:T(8,128)(2,1)S(1)} collective-permute-done((bf16[2,256,256]{1,2,0:T(8,128)(2,1)S(1)}, bf16[2,256,256]{1,2,0:T(8,128)(2,1)S(1)}, u32[]{:S(2)}, u32[]{:S(2)}) %collective-permute-start.14) | collective-permute-done | bytes 262176 | tf_op jit(solution)/shard_map/ppermute | solution.py:16
  116.9 4.2 collective-permute-done.15
  121.1 1.6 fusion.29
  122.7 2.7 copy-done.1
  125.5 2.0 fusion.2
  127.5 5.8 fusion.30
  133.3 4.4 fusion.10
  139.4 113.8 %reduce-scatter.3.cloned.1.call-done = bf16[256,256]{1,0:T(8,128)(2,1)} async-done(((bf16[256,2048]{1,0:T(8,128)(2,1)}), bf16[256,256]{1,0:T(8,128)(2,1)}) %reduce-scatter.3.cloned.1.call-update) | async-done | bytes 131088 | tf_op jit(solution)/shard_map/reduce_scatter | solution.py:88
  253.3 1.6 add_convert_fusion.1
  256.8 79.5 %all-gather.5.cloned.1.call-done = bf16[256,2048]{1,0:T(8,128)(2,1)} async-done(((bf16[256,256]{1,0:T(8,128)(2,1)}), bf16[256,2048]{1,0:T(8,128)(2,1)}) %all-gather.5.cloned.1.call-update) | async-done | bytes 1048592 | tf_op jit(solution)/shard_map/all_gather | solution.py:92
  336.3 1.6 fusion.6
  338.0 114.2 %all-gather.7.cloned.1.call-done = bf16[2048,512]{1,0:T(8,128)(2,1)} async-done(((bf16[32,512]{1,0:T(8,128)(2,1)}), bf16[2048,512]{1,0:T(8,128)(2,1)}) %all-gather.7.cloned.1.call-update) | async-done | bytes 2097168 | tf_op jit(solution)/shard_map/all_gather | solution.py:95
  452.1 2.7 fusion.18
  454.8 116.1 %all-gather.11.cloned.1.call-done = bf16[2048,512]{1,0:T(8,128)(2,1)} async-done(((bf16[32,512]{1,0:T(8,128)(2,1)}), bf16[2048,512]{1,0:T(8,128)(2,1)}) %all-gather.11.cloned.1.call-update) | async-done | bytes 2097168 | tf_op jit(solution)/shard_map/all_gather | solution.py:97
  570.9 118.8 %all-gather.9.cloned.1.call-done = bf16[2048,512]{1,0:T(8,128)(2,1)} async-done(((bf16[32,512]{1,0:T(8,128)(2,1)}), bf16[2048,512]{1,0:T(8,128)(2,1)}) %all-gather.9.cloned.1.call-update) | async-done | bytes 2097168 | tf_op jit(solution)/shard_map/all_gather | solution.py:96
  689.6 4.6 convolution_convert_fusion
  694.3 112.7 %reduce-scatter.5.cloned.1.call-done = bf16[256,256]{1,0:T(8,128)(2,1)} async-done(((bf16[256,2048]{1,0:T(8,128)(2,1)}), bf16[256,256]{1,0:T(8,128)(2,1)}) %reduce-scatter.5.cloned.1.call-update) | async-done | bytes 131088 | tf_op jit(solution)/shard_map/reduce_scatter | solution.py:105
  (75 shorter events, 22.9 us)
Async XLA Ops:
  6.5 131.2 %copy-start = (bf16[256,2048]{1,0:T(8,128)(2,1)S(1)}, bf16[256,2048]{1,0:T(8,128)(2,1)}, u32[]{:S(2)}) copy-start(bf16[256,2048]{1,0:T(8,128)(2,1)} %param.17) | copy-start | bytes 3145732
  6.5 246.7 %reduce-scatter.3.cloned.1.call-start = ((), (), s32[]{:S(2)}) async-start(), calls=%async_computation.2 | async-start | bytes 1179648 | tf_op jit(solution)/shard_map/reduce_scatter | solution.py:88
  8.7 44.5 %collective-permute-start = (bf16[2,256,256]{1,2,0:T(8,128)(2,1)S(1)}, bf16[2,256,256]{1,2,0:T(8,128)(2,1)}, u32[]{:S(2)}, u32[]{:S(2)}) collective-permute-start(bf16[2,256,256]{1,2,0:T(8,128)(2,1)S(1)} %pad_maximum_fusion), channel_id=1, source_target_pairs={{0,64},{8,72},{16,80},{24,88},{32,96},{40,104},{48,112},{56,120},{... | collective-permute-start | bytes 786440 | tf_op jit(solution)/shard_map/ppermute | solution.py:16
  13.8 46.1 %collective-permute-start.1 = (bf16[2,256,256]{1,2,0:T(8,128)(2,1)S(1)}, bf16[2,256,256]{1,2,0:T(8,128)(2,1)}, u32[]{:S(2)}, u32[]{:S(2)}) collective-permute-start(bf16[2,256,256]{1,2,0:T(8,128)(2,1)S(1)} %pad_maximum_fusion), channel_id=1, source_target_pairs={{0,56},{8,64},{16,72},{24,80},{32,88},{40,96},{48,104},{56,112},{6... | collective-permute-start | bytes 786440 | tf_op jit(solution)/shard_map/ppermute | solution.py:16
  18.2 45.3 %collective-permute-start.2 = (bf16[2,256,256]{1,2,0:T(8,128)(2,1)S(1)}, bf16[2,256,256]{1,2,0:T(8,128)(2,1)S(1)}, u32[]{:S(2)}, u32[]{:S(2)}) collective-permute-start(bf16[2,256,256]{1,2,0:T(8,128)(2,1)S(1)} %pad_maximum_fusion), channel_id=1, source_target_pairs={{0,48},{8,56},{16,64},{24,72},{32,80},{40,88},{48,96},{56,104},{64... | collective-permute-start | bytes 786440 | tf_op jit(solution)/shard_map/ppermute | solution.py:16
  22.1 43.9 %collective-permute-start.3 = (bf16[2,256,256]{1,2,0:T(8,128)(2,1)S(1)}, bf16[2,256,256]{1,2,0:T(8,128)(2,1)S(1)}, u32[]{:S(2)}, u32[]{:S(2)}) collective-permute-start(bf16[2,256,256]{1,2,0:T(8,128)(2,1)S(1)} %pad_maximum_fusion), channel_id=1, source_target_pairs={{0,40},{8,48},{16,56},{24,64},{32,72},{40,80},{48,88},{56,96},{64,... | collective-permute-start | bytes 786440 | tf_op jit(solution)/shard_map/ppermute | solution.py:16
  25.5 42.5 %collective-permute-start.4 = (bf16[2,256,256]{1,2,0:T(8,128)(2,1)S(1)}, bf16[2,256,256]{1,2,0:T(8,128)(2,1)S(1)}, u32[]{:S(2)}, u32[]{:S(2)}) collective-permute-start(bf16[2,256,256]{1,2,0:T(8,128)(2,1)S(1)} %pad_maximum_fusion), channel_id=1, source_target_pairs={{0,32},{8,40},{16,48},{24,56},{32,64},{40,72},{48,80},{56,88},{64,... | collective-permute-start | bytes 786440 | tf_op jit(solution)/shard_map/ppermute | solution.py:16
  53.2 16.1 %collective-permute-start.5 = (bf16[2,256,256]{1,2,0:T(8,128)(2,1)S(1)}, bf16[2,256,256]{1,2,0:T(8,128)(2,1)S(1)}, u32[]{:S(2)}, u32[]{:S(2)}) collective-permute-start(bf16[2,256,256]{1,2,0:T(8,128)(2,1)S(1)} %pad_maximum_fusion), channel_id=1, source_target_pairs={{0,24},{8,32},{16,40},{24,48},{32,56},{40,64},{48,72},{56,80},{64,... | collective-permute-start | bytes 786440 | tf_op jit(solution)/shard_map/ppermute | solution.py:16
  59.8 10.8 %collective-permute-start.6 = (bf16[2,256,256]{1,2,0:T(8,128)(2,1)S(1)}, bf16[2,256,256]{1,2,0:T(8,128)(2,1)S(1)}, u32[]{:S(2)}, u32[]{:S(2)}) collective-permute-start(bf16[2,256,256]{1,2,0:T(8,128)(2,1)S(1)} %pad_maximum_fusion), channel_id=1, source_target_pairs={{0,16},{8,24},{16,32},{24,40},{32,48},{40,56},{48,64},{56,72},{64,... | collective-permute-start | bytes 786440 | tf_op jit(solution)/shard_map/ppermute | solution.py:16
  63.4 8.5 %collective-permute-start.7 = (bf16[2,256,256]{1,2,0:T(8,128)(2,1)S(1)}, bf16[2,256,256]{1,2,0:T(8,128)(2,1)S(1)}, u32[]{:S(2)}, u32[]{:S(2)}) collective-permute-start(bf16[2,256,256]{1,2,0:T(8,128)(2,1)S(1)} %pad_maximum_fusion), channel_id=1, source_target_pairs={{0,8},{8,16},{16,24},{24,32},{32,40},{40,48},{48,56},{56,64},{64,7... | collective-permute-start | bytes 786440 | tf_op jit(solution)/shard_map/ppermute | solution.py:16
  66.0 8.9 %collective-permute-start.8 = (bf16[2,256,256]{1,2,0:T(8,128)(2,1)S(1)}, bf16[2,256,256]{1,2,0:T(8,128)(2,1)S(1)}, u32[]{:S(2)}, u32[]{:S(2)}) collective-permute-start(bf16[2,256,256]{1,2,0:T(8,128)(2,1)S(1)} %pad_maximum_fusion), channel_id=1, source_target_pairs={{8,0},{16,8},{24,16},{32,24},{40,32},{48,40},{56,48},{64,56},{72,6... | collective-permute-start | bytes 786440 | tf_op jit(solution)/shard_map/ppermute | solution.py:16
  67.9 10.4 %collective-permute-start.9 = (bf16[2,256,256]{1,2,0:T(8,128)(2,1)S(1)}, bf16[2,256,256]{1,2,0:T(8,128)(2,1)S(1)}, u32[]{:S(2)}, u32[]{:S(2)}) collective-permute-start(bf16[2,256,256]{1,2,0:T(8,128)(2,1)S(1)} %pad_maximum_fusion), channel_id=1, source_target_pairs={{16,0},{24,8},{32,16},{40,24},{48,32},{56,40},{64,48},{72,56},{80,... | collective-permute-start | bytes 786440 | tf_op jit(solution)/shard_map/ppermute | solution.py:16
  69.3 11.7 %collective-permute-start.10 = (bf16[2,256,256]{1,2,0:T(8,128)(2,1)S(1)}, bf16[2,256,256]{1,2,0:T(8,128)(2,1)S(1)}, u32[]{:S(2)}, u32[]{:S(2)}) collective-permute-start(bf16[2,256,256]{1,2,0:T(8,128)(2,1)S(1)} %pad_maximum_fusion), channel_id=1, source_target_pairs={{24,0},{32,8},{40,16},{48,24},{56,32},{64,40},{72,48},{80,56},{88,... | collective-permute-start | bytes 786440 | tf_op jit(solution)/shard_map/ppermute | solution.py:16
  70.6 13.6 %collective-permute-start.11 = (bf16[2,256,256]{1,2,0:T(8,128)(2,1)S(1)}, bf16[2,256,256]{1,2,0:T(8,128)(2,1)S(1)}, u32[]{:S(2)}, u32[]{:S(2)}) collective-permute-start(bf16[2,256,256]{1,2,0:T(8,128)(2,1)S(1)} %pad_maximum_fusion), channel_id=1, source_target_pairs={{32,0},{40,8},{48,16},{56,24},{64,32},{72,40},{80,48},{88,56},{96,... | collective-permute-start | bytes 786440 | tf_op jit(solution)/shard_map/ppermute | solution.py:16
  72.0 18.7 %collective-permute-start.12 = (bf16[2,256,256]{1,2,0:T(8,128)(2,1)S(1)}, bf16[2,256,256]{1,2,0:T(8,128)(2,1)S(1)}, u32[]{:S(2)}, u32[]{:S(2)}) collective-permute-start(bf16[2,256,256]{1,2,0:T(8,128)(2,1)S(1)} %pad_maximum_fusion), channel_id=1, source_target_pairs={{40,0},{48,8},{56,16},{64,24},{72,32},{80,40},{88,48},{96,56},{104... | collective-permute-start | bytes 786440 | tf_op jit(solution)/shard_map/ppermute | solution.py:16
  74.9 16.0 %collective-permute-start.13 = (bf16[2,256,256]{1,2,0:T(8,128)(2,1)S(1)}, bf16[2,256,256]{1,2,0:T(8,128)(2,1)S(1)}, u32[]{:S(2)}, u32[]{:S(2)}) collective-permute-start(bf16[2,256,256]{1,2,0:T(8,128)(2,1)S(1)} %pad_maximum_fusion), channel_id=1, source_target_pairs={{48,0},{56,8},{64,16},{72,24},{80,32},{88,40},{96,48},{104,56},{11... | collective-permute-start | bytes 786440 | tf_op jit(solution)/shard_map/ppermute | solution.py:16
  78.4 38.5 %collective-permute-start.14 = (bf16[2,256,256]{1,2,0:T(8,128)(2,1)S(1)}, bf16[2,256,256]{1,2,0:T(8,128)(2,1)S(1)}, u32[]{:S(2)}, u32[]{:S(2)}) collective-permute-start(bf16[2,256,256]{1,2,0:T(8,128)(2,1)S(1)} %pad_maximum_fusion), channel_id=1, source_target_pairs={{56,0},{64,8},{72,16},{80,24},{88,32},{96,40},{104,48},{112,56},{1... | collective-permute-start | bytes 786440 | tf_op jit(solution)/shard_map/ppermute | solution.py:16
  81.0 40.0 %collective-permute-start.15 = (bf16[2,256,256]{1,2,0:T(8,128)(2,1)S(1)}, bf16[2,256,256]{1,2,0:T(8,128)(2,1)S(1)}, u32[]{:S(2)}, u32[]{:S(2)}) collective-permute-start(bf16[2,256,256]{1,2,0:T(8,128)(2,1)S(1)} %pad_maximum_fusion), channel_id=1, source_target_pairs={{64,0},{72,8},{80,16},{88,24},{96,32},{104,40},{112,48},{120,56},{... | collective-permute-start | bytes 786440 | tf_op jit(solution)/shard_map/ppermute | solution.py:16
  121.1 1.7 copy-start.5
  121.1 4.4 copy-start.1
  127.5 5.8 copy-start.2
  133.3 120.0 %copy-start.6 = (bf16[256,256]{1,0:T(8,128)(2,1)S(1)}, bf16[256,256]{1,0:T(8,128)(2,1)}, u32[]{:S(2)}) copy-start(bf16[256,256]{1,0:T(8,128)(2,1)} %param.14) | copy-start | bytes 393220
  137.7 314.4 %copy-start.7 = (f32[2048]{0:T(1024)S(1)}, f32[2048]{0:T(1024)}, u32[]{:S(2)}) copy-start(f32[2048]{0:T(1024)} %param.21) | copy-start | bytes 24580
  139.2 197.1 %all-gather.5.cloned.1.call-start = ((), (), s32[]{:S(2)}) async-start(), calls=%async_computation.3 | async-start | bytes 1179648 | tf_op jit(solution)/shard_map/all_gather | solution.py:92
  254.9 197.2 %all-gather.7.cloned.1.call-start = ((), (), s32[]{:S(2)}) async-start(), calls=%async_computation.4 | async-start | bytes 2129920 | tf_op jit(solution)/shard_map/all_gather | solution.py:95
  255.6 315.3 %all-gather.11.cloned.1.call-start = ((), (), s32[]{:S(2)}) async-start(), calls=%async_computation.6 | async-start | bytes 2129920 | tf_op jit(solution)/shard_map/all_gather | solution.py:97
  256.2 433.4 %all-gather.9.cloned.1.call-start = ((), (), s32[]{:S(2)}) async-start(), calls=%async_computation.5 | async-start | bytes 2129920 | tf_op jit(solution)/shard_map/all_gather | solution.py:96
  256.8 550.2 %reduce-scatter.5.cloned.1.call-start = ((), (), s32[]{:S(2)}) async-start(), calls=%async_computation.7 | async-start | bytes 1179648 | tf_op jit(solution)/shard_map/reduce_scatter | solution.py:105
  336.3 353.3 %copy-start.4 = (bf16[256,2048]{1,0:T(8,128)(2,1)S(1)}, bf16[256,2048]{1,0:T(8,128)(2,1)}, u32[]{:S(2)}) copy-start(bf16[256,2048]{1,0:T(8,128)(2,1)} %all-gather.5.cloned.1.call-done) | copy-start | bytes 3145732
  454.8 352.2 %copy-start.3 = (bf16[256,256]{1,0:T(8,128)(2,1)S(1)}, bf16[256,256]{1,0:T(8,128)(2,1)}, u32[]{:S(2)}) copy-start(bf16[256,256]{1,0:T(8,128)(2,1)} %add_convert_fusion.1) | copy-start | bytes 393220
Sparse Core Ops, SparseCore 0:
  139.3 113.8 reduce-scatter.2
  256.8 79.5 all-gather.4
  338.7 113.3 all-gather.6
  454.3 116.4 all-gather.10
  573.1 116.4 all-gather.8
  694.7 112.2 reduce-scatter.4
where the time goes:
time: 817 us; the launch traced here: 815 us
  waiting for transfers between devices  700 us (86%)
  starting transfers between devices  43.4 us (5%)
  local copies, waits for them, and re-layouts  27 us (3%)
  matrix products  16.3 us (2%)
  other arithmetic  14.4 us (2%)
  between operations  13.9 us (2%)
    all_gather x1, waiting for transfers between devices, shards(): lax.all_gather(up_weight, 'seq', axis=0, tiled=True)  119 us
    all_gather x1, waiting for transfers between devices, shards(): lax.all_gather(down_weight_t, 'seq', axis=0, tiled=True)  116 us
    all_gather x1, waiting for transfers between devices, shards(): lax.all_gather(gate_weight, 'seq', axis=0, tiled=True)  114 us
    reduce_scatter x1, waiting for transfers between devices, shards(): lax.psum_scatter(partial_value.astype(jnp.bfloat16), 'tp', scatter_dimens...  114 us
    reduce_scatter x1, waiting for transfers between devices, shards(): lax.psum_scatter(terms.astype(jnp.bfloat16), 'tp', scatter_dimension=1, t...  113 us
    all_gather x1, waiting for transfers between devices, shards(): full_state = lax.all_gather(own_state, 'tp', axis=1, tiled=True)  79.5 us
    ppermute x16, waiting for transfers between devices, shifted(): return lax.ppermute(x, axis, pairs)  43.7 us
    ppermute x16, starting transfers between devices, shifted(): return lax.ppermute(x, axis, pairs)  43 us
  transfers between devices with their start and end apart: 22, of which 14 were waited for; matrix products, arithmetic and copies ran while one was open for 4% of the time, Pallas kernels for 0%

commit v1 on v0

v1 whole, which is shorter than its diff:
```python
import jax
import jax.numpy as jnp
from jax import lax
from jax.experimental import pallas as pl
from jax.experimental.pallas import tpu as pltpu
from jax.sharding import PartitionSpec as P

HEAD_DIM = 128
TILE = 128
HALF_BAND = 2048
OFFSETS = 33
NZ = 8
NY = 4
NX = 4
CHIPS = NZ * NY
ROWS = 256
COLS = 256
FFB = 512
WROWS = 32
SCALE = HEAD_DIM ** (-0.5)
MESH = pl.DeviceIdType.MESH
F32 = jnp.float32
BF16 = jnp.bfloat16


def remote(src, dst, send_sem, recv_sem, dev):
    return pltpu.make_async_remote_copy(
        src_ref=src,
        dst_ref=dst,
        send_sem=send_sem,
        recv_sem=recv_sem,
        device_id=dev,
        device_id_type=MESH,
    )


class Place:
    def __init__(self):
        s = lax.axis_index("seq")
        t = lax.axis_index("tp")
        self.s, self.t = s, t
        self.c = lax.rem(s, 2)
        self.chip = s // 2
        self.y = lax.rem(self.chip, NY)
        self.z = self.chip // NY
        self.x = lax.rem(t, NX)
        self.h = t // NX
        self.sib = (s + 1 - 2 * self.c, t)
        self.yp = lax.rem(self.y + 1, NY)
        self.ym = lax.rem(self.y + 3, NY)
        self.y2 = lax.rem(self.y + 2, NY)
        self.dyp = self.dev(self.z, self.yp)
        self.dym = self.dev(self.z, self.ym)
        self.dy2 = self.dev(self.z, self.y2)
        self.dzp = self.dev(self.z + 1, self.y)
        self.dzm = self.dev(self.z - 1, self.y)
        self.dx = [None] + [(s, self.h * NX + lax.rem(self.x + d, NX)) for d in (1, 2, 3)]
        self.far = (s, (1 - self.h) * NX + self.x)
        zz = self.h * NZ + self.z
        self.dq = []
        for step in (4, 12):
            zq = lax.rem(zz + step, 2 * NZ)
            seq = ((lax.rem(zq, NZ)) * NY + self.y) * 2 + self.c
            self.dq.append((seq, (zq // NZ) * NX + self.x))

    def dev(self, z, y):
        return ((z * NY + y) * 2 + self.c, self.t)


class Gather:
    def __init__(self, at, buf, half, rs, rb, zs, ys, bs):
        self.at, self.buf, self.half = at, buf, half
        self.rs, self.rb, self.zs, self.ys, self.bs = rs, rb, zs, ys, bs

    def full(self, chip, sem, core, send_sem, dev):
        slot = self.buf.at[chip * 2 + core]
        return remote(slot, slot, send_sem, sem, dev)

    def part(self, chip, i, send_sem, dev):
        slot = self.buf.at[chip * 2 + self.at.c, pl.ds(i * self.half, self.half)]
        return remote(slot, slot, send_sem, self.rs.at[chip, i], dev)

    def sib(self, chip):
        return self.full(chip, self.rb.at[chip], self.at.c, self.bs.at[chip], self.at.sib)

    def zstep(self, k, go=True):
        at = self.at
        for way, origin, nxt, dev in (
            (0, at.z - k, at.z + 1, at.dzp),
            (1, at.z + k, at.z - 1, at.dzm),
        ):
            chip = origin * NY + at.y
            valid = jnp.logical_and(origin >= 0, origin < NZ)
            d = self.full(chip, self.rs.at[chip, 0], at.c, self.zs.at[chip, way], dev)

            @pl.when(valid)
            def _(d=d, nxt=nxt):
                if go and not (isinstance(k, int) and k == 0):
                    d.wait_recv()

                @pl.when(jnp.logical_and(nxt >= 0, nxt < NZ))
                def _():
                    if go:
                        d.start()
                    else:
                        d.wait_send()

    def each(self, k, f):
        at = self.at

        @pl.when(at.z - k >= 0)
        def _():
            f(at.z - k)

        @pl.when(jnp.logical_and(k > 0, at.z + k < NZ))
        def _():
            f(at.z + k)

    def ysend(self, k, go=True):
        at = self.at

        def f(zo):
            chip = zo * NY + at.y
            for i, dev in ((0, at.dyp), (1, at.dym)):
                d = self.full(chip, self.rs.at[chip, 0], at.c, self.ys.at[chip, i], dev)
                d.start() if go else d.wait_send()
            d = self.sib(chip)
            d.start() if go else d.wait_send()

        self.each(k, f)

    def yrecv(self, k, go=True):
        at = self.at

        def f(zo):
            for i, yo, dev in ((0, at.ym, at.dyp), (1, at.yp, at.dym)):
                chip = zo * NY + yo
                if go:
                    self.full(chip, self.rs.at[chip, 0], at.c, self.bs.at[chip], at.sib).wait_recv()
                r = self.part(chip, i, self.ys.at[chip, i], dev)
                d = self.sib(chip)
                if go:
                    r.start()
                    d.start()
                else:
                    r.wait_send()
                    d.wait_send()
            chip = zo * NY + at.y2
            d = self.sib(chip)
            if go:
                for i in (0, 1):
                    self.part(chip, i, self.bs.at[chip], at.sib).wait_recv()
                d.start()
            else:
                d.wait_send()

        self.each(k, f)

    def wait_other_core(self):
        at = self.at

        @pl.loop(0, CHIPS)
        def _(chip):
            self.full(chip, self.rb.at[chip], 1 - at.c, self.bs.at[chip], at.sib).wait_recv()


class Cross:
    def __init__(self, at, src, rel, dst, s1, r1, s2, r2):
        self.at = at
        self.first = [remote(src[i], rel[i], s1.at[i], r1.at[i], at.dq[i]) for i in (0, 1)]
        self.second = [remote(rel[i], dst[i], s2.at[i], r2.at[i], at.dq[i]) for i in (0, 1)]

    def send(self, i):
        self.first[i].start()

    def relay(self):
        for i in (0, 1):
            self.first[i].wait_recv()
            self.second[i].start()

    def wait(self):
        for i in (0, 1):
            self.second[i].wait_recv()

    def drain(self):
        for i in (0, 1):
            self.first[i].wait_send()
            self.second[i].wait_send()


def kernel(
    q_ref, res_ref, tab_ref, bk_ref, gain_ref, k_hbm, v_hbm, wo_hbm, g_hbm, u_hbm, d_hbm,
    out_ref,
    kvb, wbuf, wob, wo_own, att_own, att_rel, att_oth, res_rel, res_oth,
    m_ref, l_ref, acc_ref, part_ref, rs_s, rs_r, rs2_s, rs2_r, st_ref, fin_s, fin_rel, fin_r,
    keep_ref,
    loc, kv_r, kv_b, kv_s, kv_s2, kv_bs,
    w_rs, w_rb, w_zs, w_ys, w_bs, o_rs, o_rb, o_zs, o_ys, o_bs, o_far,
    x1_s, x1_r, x2_s, x2_r, x3_s, x3_r, ca, cr, cf,
):
    at = Place()
    s, c, x, h, y, z = at.s, at.c, at.x, at.h, at.y, at.z

    loads = [
        pltpu.make_async_copy(k_hbm, kvb.at[4, c, 0], loc.at[0]),
        pltpu.make_async_copy(v_hbm, kvb.at[4, c, 1], loc.at[1]),
        pltpu.make_async_copy(g_hbm, wbuf.at[s, pl.ds(0, WROWS)], loc.at[2]),
        pltpu.make_async_copy(u_hbm, wbuf.at[s, pl.ds(WROWS, WROWS)], loc.at[3]),
        pltpu.make_async_copy(d_hbm, wbuf.at[s, pl.ds(2 * WROWS, WROWS)], loc.at[4]),
        pltpu.make_async_copy(wo_hbm, wo_own, loc.at[5]),
    ]
    for d in loads:
        d.start()

    barrier = pltpu.get_barrier_semaphore()
    peers = [at.sib, at.dyp, at.dym, at.dy2, at.far] + at.dx[1:] + at.dq
    for dev in peers:
        pl.semaphore_signal(barrier, inc=1, device_id=dev, device_id_type=MESH)

    @pl.when(z < NZ - 1)
    def _():
        pl.semaphore_signal(barrier, inc=1, device_id=at.dzp, device_id_type=MESH)

    @pl.when(z > 0)
    def _():
        pl.semaphore_signal(barrier, inc=1, device_id=at.dzm, device_id_type=MESH)

    pl.semaphore_wait(barrier, len(peers) + (1 - (z + 1) // NZ) + (z + NZ - 1) // NZ)
    loads[0].wait()
    loads[1].wait()

    top = (y + 1) // 4
    low = 1 - (y + 3) // 4
    upper = y // 2
    lp, lm, l2 = 1 - 4 * top, 4 * low - 1, 2 - 4 * upper

    def kv_copy(o, to, send_sem, dev):
        return remote(kvb.at[o + 4, c], kvb.at[to + 4, c], send_sem, kv_r.at[to + 4], dev)

    def kv_sib(o):
        return remote(kvb.at[o + 4, c], kvb.at[o + 4, c], kv_bs.at[o + 4], kv_b.at[o + 4], at.sib)

    kz = [(kv_copy(0, -4, kv_s.at[0], at.dzp), z < NZ - 1), (kv_copy(0, 4, kv_s.at[1], at.dzm), z > 0)]
    ky = [
        kv_copy(0, -lp, kv_s.at[2], at.dyp),
        kv_copy(0, -lm, kv_s.at[3], at.dym),
        kv_copy(0, -l2, kv_s.at[4], at.dy2),
    ]
    for d, ok in kz:
        pl.when(ok)(d.start)
    for d in ky:
        d.start()
    kv_sib(0).start()

    cross_r = Cross(
        at,
        [res_ref.at[pl.ds(128 * i, 128)] for i in (0, 1)],
        [res_rel.at[i] for i in (0, 1)],
        [res_oth.at[pl.ds(128 * i, 128)] for i in (0, 1)],
        *[cr.at[i] for i in range(4)],
    )
    cross_r.send(0)
    cross_r.send(1)
    piece = []
    for i in (0, 1):
        rows = pl.ds(pl.multiple_of(16 * (s // 4), 16), 16)
        cols = pl.ds(pl.multiple_of(1024 * i + 256 * lax.rem(s, 4), 256), 256)
        piece.append(remote(wo_hbm.at[rows, cols], wob.at[s, i], o_far.at[0, i], o_far.at[1, i], at.far))
    for d in piece:
        d.start()

    gw = Gather(at, wbuf, 48, w_rs, w_rb, w_zs, w_ys, w_bs)
    go = Gather(at, wob, 1, o_rs, o_rb, o_zs, o_ys, o_bs)

    m_ref[...] = jnp.full(m_ref.shape, -1e30, F32)
    l_ref[...] = jnp.zeros(l_ref.shape, F32)
    acc_ref[...] = jnp.zeros(acc_ref.shape, F32)

    def update(i, sc, v):
        m_old = m_ref[i]
        m_new = jnp.maximum(m_old, jnp.max(sc, axis=1, keepdims=True))
        alpha = jnp.exp(m_old - m_new)
        p = jnp.exp(sc - m_new[:, 0:1])
        l_ref[i] = alpha * l_ref[i] + jnp.sum(p, axis=1, keepdims=True)
        pv = jnp.dot(p.astype(BF16), v, preferred_element_type=F32)
        acc_ref[i] = alpha * acc_ref[i] + pv
        m_ref[i] = m_new

    def bias_of(i, first, kt):
        idx = first + kt - lax.rem(i, 2) + HALF_BAND // TILE
        idx = jnp.clip(idx, 0, OFFSETS - 1)
        return tab_ref[i // 2, bk_ref[lax.rem(i, 2), idx]]

    def attend(o, core=None):
        @pl.loop(0, 4)
        def _(i):
            head = pl.ds(pl.multiple_of(128 * (i // 2), 128), 128)
            q = q_ref[pl.ds(pl.multiple_of(128 * lax.rem(i, 2), 128), 128), head]
            if core is None:
                n = 512
                k = kvb[o + 4, :, 0, :, head].reshape(n, 128)
                v = kvb[o + 4, :, 1, :, head].reshape(n, 128)
                first = 4 * o - 2 * c
            else:
                n = 256
                k = kvb[o + 4, core, 0, :, head]
                v = kvb[o + 4, core, 1, :, head]
                first = 4 * o + 2 * core - 2 * c
            sc = lax.dot_general(q, k, (((1,), (1,)), ((), ())), preferred_element_type=F32)
            sc = jnp.concatenate(
                [sc[:, 128 * kt : 128 * kt + 128] * SCALE + bias_of(i, first, kt) for kt in range(n // 128)],
                axis=1,
            )
            if core is not None:
                row = lax.broadcasted_iota(jnp.int32, sc.shape, 0)
                col = lax.broadcasted_iota(jnp.int32, sc.shape, 1)
                dist = col - row + (first - lax.rem(i, 2)) * TILE
                sc = jnp.where(jnp.abs(dist) <= HALF_BAND, sc, -1e30)
            update(i, sc, v)

    def inside(o):
        return jnp.logical_and(at.chip + o >= 0, at.chip + o < CHIPS)

    def got_own(o):
        kv_copy(o, o, kv_bs.at[0], at.sib).wait_recv()

    def got_sib(o):
        d = remote(kvb.at[o + 4, 1 - c], kvb.at[o + 4, 1 - c], kv_bs.at[o + 4], kv_b.at[o + 4], at.sib)
        d.wait_recv()

    for d in loads[2:5]:
        d.wait()
    gw.zstep(0)
    got_sib(0)
    attend(0)

    second = []
    for i, (delta, sgn, dev) in enumerate(
        ((lp, 1 - 2 * top, at.dyp), (lm, 2 * low - 1, at.dym), (l2, 1 - 2 * upper, at.dy2))
    ):
        src = 4 * sgn
        second.append((kv_copy(src, src - delta, kv_s2.at[i], dev), inside(src)))
    for o in (-4, 4):
        pl.when(inside(o))(lambda o=o: got_own(o))
    for d, ok in second:
        pl.when(ok)(d.start)
    for o, keep in ((-4, 1), (4, 0)):
        pl.when(jnp.logical_and(inside(o), c == keep))(lambda o=o: kv_sib(o).start())
    gw.zstep(1)
    cross_r.relay()
    for i in (0, 1):
        piece[i].wait_recv()
    go.zstep(0)
    go.ysend(0)
    for o, core in ((-4, 0), (-4, 1), (4, 0), (4, 1)):
        need = inside(o)
        if (o, core) == (-4, 0):
            need = jnp.logical_and(need, c == 0)
        if (o, core) == (4, 1):
            need = jnp.logical_and(need, c == 1)

        @pl.when(need)
        def _(o=o, core=core):
            @pl.when(c != core)
            def _():
                got_sib(o)

            attend(o, core)

    wave1 = [4 * low - 1, 1 - 4 * top, 2 - 4 * upper]
    wave2 = [2 - wave1[0], -2 - wave1[1], -wave1[2]]
    for o in wave1:
        got_own(o)
        kv_sib(o).start()
    gw.zstep(2)
    go.zstep(1)
    for n, o in enumerate(wave1):
        got_sib(o)
        attend(o)
        go.zstep(2 + n)
        if n == 1:
            gw.zstep(3)
    for o in wave2:

        @pl.when(inside(o))
        def _(o=o):
            got_own(o)
            kv_sib(o).start()

    gw.zstep(4)
    for n, o in enumerate(wave2):

        @pl.when(inside(o))
        def _(o=o):
            got_sib(o)
            attend(o)

        go.zstep(5 + n)

    for i in range(4):
        hd, a = i // 2, i % 2
        att_own[hd, pl.ds(128 * a, 128), :] = (acc_ref[i] / l_ref[i]).astype(BF16)
    cross_a = Cross(
        at,
        [att_own.at[i] for i in (0, 1)],
        [att_rel.at[i] for i in (0, 1)],
        [att_oth.at[i] for i in (0, 1)],
        *[ca.at[i] for i in range(4)],
    )
    cross_a.send(0)
    cross_a.send(1)

    @pl.loop(1, NZ)
    def _(k):
        go.ysend(k)

    gw.ysend(0)
    loads[5].wait()
    att = jnp.concatenate([att_own[0], att_own[1]], axis=1)
    order = (2, 1, 3, 0)

    def colsof(d, i):
        xd = lax.rem(x + d, NX)
        return pl.ds(pl.multiple_of(1024 * i + 256 * xd, 256), 256)

    @pl.loop(0, 4)
    def _(d):
        for i in (0, 1):
            part_ref[d, :, pl.ds(256 * i, 256)] = jnp.dot(att, wo_own[:, colsof(d, i)], preferred_element_type=F32)

    @pl.loop(0, NZ)
    def _(k):
        go.yrecv(k)

    cross_a.relay()
    gw.zstep(5)
    go.wait_other_core()
    gw.zstep(6)
    gw.zstep(7)

    @pl.loop(1, NZ)
    def _(k):
        gw.ysend(k)

    cross_a.wait()
    oth = jnp.concatenate([att_oth[0], att_oth[1]], axis=1)
    wob4 = wob.reshape(16, 4, 2, 16, 256)
    rs = [remote(rs_s.at[d - 1], rs_r.at[d - 1], x1_s.at[d - 1], x1_r.at[d - 1], at.dx[d]) for d in (1, 2, 3)]
    for d in order:
        xd = lax.rem(x + d, NX)
        for i in (0, 1):
            w = wob4[:, xd, i].reshape(256, 256)
            cols = pl.ds(256 * i, 256)
            p = part_ref[d, :, cols] + jnp.dot(oth, w, preferred_element_type=F32)
            if d:
                rs_s[d - 1, :, cols] = p.astype(BF16)
            else:
                part_ref[0, :, cols] = p
        if d:
            rs[d - 1].start()

    cross_r.wait()
    for d in rs:
        d.wait_recv()
    own = h == 0
    res0, res1 = res_ref[...].astype(F32), res_oth[...].astype(F32)
    for i in (0, 1):
        cols = pl.ds(256 * i, 256)
        r = jnp.where(own, res0, res1) if i == 0 else jnp.where(own, res1, res0)
        tot = part_ref[0, :, cols] + r
        for d in (1, 2, 3):
            tot += rs_r[d - 1, :, cols].astype(F32)
        st_ref[x, :, cols] = tot.astype(BF16)
    ag = [remote(st_ref.at[x], st_ref.at[x], x2_s.at[d - 1], x2_r.at[d - 1], at.dx[d]) for d in (1, 2, 3)]
    for d in (2, 1, 3):
        ag[d - 1].start()

    @pl.loop(0, NZ)
    def _(k):
        gw.yrecv(k)

    gw.wait_other_core()
    for d in (1, 2, 3):
        xo = lax.rem(x + 4 - d, NX)
        remote(st_ref.at[xo], st_ref.at[xo], x2_s.at[d - 1], x2_r.at[d - 1], at.dx[d]).wait_recv()

    ssq = jnp.zeros((ROWS, 1), F32)
    for xo in range(NX):
        w = st_ref[xo].astype(F32)
        ssq += jnp.sum(w * w, axis=1, keepdims=True)
    scale = lax.rsqrt(ssq / 2048.0 + 1e-05)
    gate = jnp.zeros((ROWS, FFB), F32)
    up = jnp.zeros((ROWS, FFB), F32)
    for b in range(8):
        hb, xb = b // 4, b % 4
        blk = st_ref[xb, :, 256 * hb : 256 * hb + 256].astype(F32)
        nb = (blk * scale * gain_ref[:, 256 * b : 256 * b + 256]).astype(BF16)
        gate += jnp.dot(nb, wbuf[8 * b : 8 * b + 8, 0:WROWS, :].reshape(256, FFB), preferred_element_type=F32)
        up += jnp.dot(nb, wbuf[8 * b : 8 * b + 8, WROWS : 2 * WROWS, :].reshape(256, FFB), preferred_element_type=F32)
    hidden = (gate / (1.0 + jnp.exp(-gate)) * up).astype(BF16)

    rs2 = [remote(rs2_s.at[d - 1], rs2_r.at[d - 1], x3_s.at[d - 1], x3_r.at[d - 1], at.dx[d]) for d in (1, 2, 3)]
    for d in order:
        xd = lax.rem(x + d, NX)
        for i in (0, 1):
            w = wbuf[pl.ds(8 * (4 * i + xd), 8), 2 * WROWS : 3 * WROWS, :].reshape(256, FFB)
            p = lax.dot_general(hidden, w, (((1,), (1,)), ((), ())), preferred_element_type=F32)
            cols = pl.ds(256 * i, 256)
            if d:
                rs2_s[d - 1, :, cols] = p.astype(BF16)
            else:
                part_ref[0, :, cols] = p
        if d:
            rs2[d - 1].start()
    for d in rs2:
        d.wait_recv()
    mine = pl.ds(pl.multiple_of(256 * h, 256), 256)
    theirs = pl.ds(pl.multiple_of(256 * (1 - h), 256), 256)

    def total(cols):
        tot = part_ref[0, :, cols]
        for d in (1, 2, 3):
            tot += rs2_r[d - 1, :, cols].astype(F32)
        return tot

    out_part = total(theirs).astype(BF16)
    cross_f = Cross(
        at,
        [fin_s.at[i] for i in (0, 1)],
        [fin_rel.at[i] for i in (0, 1)],
        [fin_r.at[i] for i in (0, 1)],
        *[cf.at[i] for i in range(4)],
    )
    for i in (0, 1):
        fin_s[i] = out_part[128 * i : 128 * i + 128]
        cross_f.send(i)
    keep_ref[...] = total(mine) + st_ref[x, :, mine].astype(F32)
    cross_f.relay()

    for d, ok in kz + second:
        pl.when(ok)(d.wait_send)
    for d in ky + piece + rs + ag + rs2:
        d.wait_send()
    kv_sib(0).wait_send()
    for o in wave1:
        kv_sib(o).wait_send()
    for o in wave2:
        pl.when(inside(o))(lambda o=o: kv_sib(o).wait_send())
    for o, keep in ((-4, 1), (4, 0)):
        pl.when(jnp.logical_and(inside(o), c == keep))(lambda o=o: kv_sib(o).wait_send())

    @pl.loop(0, NZ)
    def _(k):
        for g in (gw, go):
            g.zstep(k, go=False)
            g.ysend(k, go=False)
            g.yrecv(k, go=False)

    cross_r.drain()
    cross_a.drain()
    cross_f.wait()
    for i in (0, 1):
        rows = pl.ds(128 * i, 128)
        out_ref[rows, :] = (keep_ref[rows, :] + fin_r[i].astype(F32)).astype(BF16)
    cross_f.drain()


def shards(queries, keys, values, residual_in, bias_table, buckets, out_weight, gate_weight, up_weight, down_weight_t, norm_gain):
    vmem = pl.BlockSpec(memory_space=pltpu.VMEM)
    smem = pl.BlockSpec(memory_space=pltpu.SMEM)
    hbm = pl.BlockSpec(memory_space=pl.ANY)
    dma = pltpu.SemaphoreType.DMA
    v = pltpu.VMEM
    gather_sems = [dma((CHIPS, 2)), dma((CHIPS,)), dma((CHIPS, 2)), dma((CHIPS, 2)), dma((CHIPS,))]
    scratch = [
        v((9, 2, 2, ROWS, COLS), BF16),
        v((64, 96, FFB), BF16),
        v((64, 2, 16, 256), BF16),
        v((256, 2048), BF16),
        v((2, ROWS, 128), BF16),
        v((2, ROWS, 128), BF16),
        v((2, ROWS, 128), BF16),
        v((2, 128, COLS), BF16),
        v((ROWS, COLS), BF16),
        v((4, 128, 128), F32),
        v((4, 128, 128), F32),
        v((4, 128, 128), F32),
        v((4, ROWS, 512), F32),
        v((3, ROWS, 512), BF16),
        v((3, ROWS, 512), BF16),
        v((3, ROWS, 512), BF16),
        v((3, ROWS, 512), BF16),
        v((NX, ROWS, 512), BF16),
        v((2, 128, COLS), BF16),
        v((2, 128, COLS), BF16),
        v((2, 128, COLS), BF16),
        v((ROWS, COLS), F32),
        dma((6,)), dma((9,)), dma((9,)), dma((5,)), dma((3,)), dma((9,)),
        *gather_sems,
        *gather_sems,
        dma((2, 2)),
        dma((3,)), dma((3,)), dma((3,)), dma((3,)), dma((3,)), dma((3,)),
        dma((4, 2)), dma((4, 2)), dma((4, 2)),
    ]
    return pl.pallas_call(
        kernel,
        out_shape=jax.ShapeDtypeStruct((ROWS, COLS), BF16),
        in_specs=[vmem, vmem, smem, smem, vmem] + [hbm] * 6,
        out_specs=vmem,
        scratch_shapes=scratch,
        compiler_params=pltpu.CompilerParams(
            collective_id=0, has_side_effects=True, vmem_limit_bytes=60 * 1024 * 1024
        ),
        name="layer",
    )(
        queries, residual_in, bias_table, buckets, norm_gain.reshape(1, -1),
        keys, values, out_weight, gate_weight, up_weight, down_weight_t,
    )


def solution(mesh):
    return jax.shard_map(
        shards,
        mesh=mesh,
        in_specs=(
            P("seq", "tp"),
            P("seq", "tp"),
            P("seq", "tp"),
            P("seq", "tp"),
            P("tp", None),
            P("seq", None),
            P("tp", None),
            P("seq", "tp"),
            P("seq", "tp"),
            P("seq", "tp"),
            P(),
        ),
        out_specs=P("seq", "tp"),
        check_vma=False,
    )
```

time: 817 us -> 184 us (0.23)
  waiting for transfers between devices: 700 us -> 0 us
  Pallas kernels: 0 us -> 182 us
  starting transfers between devices: 43.4 us -> 0 us
  local copies, waits for them, and re-layouts: 27 us -> 1.57 us
  matrix products: 16.3 us -> 0 us
  other arithmetic: 14.4 us -> 0 us
  between operations: 13.9 us -> 0.01 us
    all_gather x4 -> x0, waiting for transfers between devices: 429 us -> none  [the longest x1 119 us: shards(): lax.all_gather(up_weight, 'seq', axis=0, tiled=True)]
    reduce_scatter x2 -> x0, waiting for transfers between devices: 226 us -> none  [the longest x1 114 us: shards(): lax.psum_scatter(partial_value.astype(jnp.bfloat16), 'tp', scatter_dimens...]
    pallas_call x0 -> x1, Pallas kernels: none -> 182 us  [shards(): pl.pallas_call(kernel, out_shape=jax.ShapeDtypeStruct((ROWS, COLS), BF16)...]
    ppermute x16 -> x0, waiting for transfers between devices: 43.7 us -> none  [shifted(): return lax.ppermute(x, axis, pairs)]
    ppermute x16 -> x0, starting transfers between devices: 43 us -> none  [shifted(): return lax.ppermute(x, axis, pairs)]
    add x2 -> x0, local copies, waits for them, and re-layouts: 18.2 us -> none  [attend_local(): scores.reshape(heads, tiles_q, TILE, tiles_k, TILE)]
    dot_general x7 -> x0, matrix products: 16.3 us -> none  [the longest x1 4.63 us: shards(): lax.dot_general(hidden, down_all, (((1,), (1,)), ((), ())), preferred_ele...]
  transfers between devices with their start and end apart: 22 -> 0, of which waited for: 14 -> 0; matrix products, arithmetic and copies ran while one was open for 4% -> 0% of each run, Pallas kernels for 0% -> 0%
where the time goes in v1:
time: 184 us
  Pallas kernels  182 us (99%)
    pallas_call x1, Pallas kernels, shards(): pl.pallas_call(kernel, out_shape=jax.ShapeDtypeStruct((ROWS, COLS), BF16)...  182 us

profile of v1, /device:TPU:1, one launch (start us, length us, event | category | flops | bytes accessed | tf_op | source)
XLA Modules:
  0.0 183.9 jit_solution(11908651018316750506)
XLA Ops:
  0.0 182.3 %layer.1 = bf16[256,256]{1,0:T(8,128)(2,1)} custom-call(bf16[256,256]{1,0:T(8,128)(2,1)} %q_ref.1, bf16[256,256]{1,0:T(8,128)(2,1)} %res_ref.1, f32[2,32]{1,0:T(2,128)} %tab_ref.1, s32[2,33]{1,0:T(2,128)} %bk_ref.1, f32[1,2048]{1,0:T(1,128)} %bitcast.1, bf16[256,256]{1,0:T(8,128)(2,1)} %k_hbm.1, bf16[256,256]{1,0:T(8,128)(2,1)} %v_hbm.1, ...), custom_call_target="tpu_custom_call" | custom-call | tf_op jit(solution)/shard_map/layer/pallas_call | solution.py:605
  182.3 1.6 copy.13

commit v2 on v1

v2 whole, which is shorter than its diff:
```python
import jax
import jax.numpy as jnp
from jax import lax
from jax.experimental import pallas as pl
from jax.experimental.pallas import tpu as pltpu
from jax.sharding import PartitionSpec as P

HEAD_DIM = 128
TILE = 128
HALF_BAND = 2048
OFFSETS = 33
NZ = 8
NY = 4
NX = 4
CHIPS = NZ * NY
ROWS = 256
COLS = 256
FFB = 512
WROWS = 32
SCALE = HEAD_DIM ** (-0.5)
LOG2E = 1.4426950408889634
MESH = pl.DeviceIdType.MESH
F32 = jnp.float32
BF16 = jnp.bfloat16


def remote(src, dst, send_sem, recv_sem, dev):
    return pltpu.make_async_remote_copy(
        src_ref=src,
        dst_ref=dst,
        send_sem=send_sem,
        recv_sem=recv_sem,
        device_id=dev,
        device_id_type=MESH,
    )


class Place:
    def __init__(self):
        s = lax.axis_index("seq")
        t = lax.axis_index("tp")
        self.s, self.t = s, t
        self.c = lax.rem(s, 2)
        self.chip = s // 2
        self.y = lax.rem(self.chip, NY)
        self.z = self.chip // NY
        self.x = lax.rem(t, NX)
        self.h = t // NX
        self.sib = (s + 1 - 2 * self.c, t)
        self.yp = lax.rem(self.y + 1, NY)
        self.ym = lax.rem(self.y + 3, NY)
        self.y2 = lax.rem(self.y + 2, NY)
        self.dyp = self.dev(self.z, self.yp)
        self.dym = self.dev(self.z, self.ym)
        self.dy2 = self.dev(self.z, self.y2)
        self.dzp = self.dev(self.z + 1, self.y)
        self.dzm = self.dev(self.z - 1, self.y)
        self.dx = [None] + [(s, self.h * NX + lax.rem(self.x + d, NX)) for d in (1, 2, 3)]
        self.far = (s, (1 - self.h) * NX + self.x)

    def dev(self, z, y):
        return ((z * NY + y) * 2 + self.c, self.t)


class Gather:
    def __init__(self, at, buf, half, rs, rb, zs, ys, bs):
        self.at, self.buf, self.half = at, buf, half
        self.rs, self.rb, self.zs, self.ys, self.bs = rs, rb, zs, ys, bs

    def full(self, chip, sem, core, send_sem, dev):
        slot = self.buf.at[chip * 2 + core]
        return remote(slot, slot, send_sem, sem, dev)

    def part(self, chip, i, send_sem, dev):
        slot = self.buf.at[chip * 2 + self.at.c, pl.ds(i * self.half, self.half)]
        return remote(slot, slot, send_sem, self.rs.at[chip, i], dev)

    def sib(self, chip):
        return self.full(chip, self.rb.at[chip], self.at.c, self.bs.at[chip], self.at.sib)

    def zstep(self, k, go=True):
        at = self.at
        for way, origin, nxt, dev in (
            (0, at.z - k, at.z + 1, at.dzp),
            (1, at.z + k, at.z - 1, at.dzm),
        ):
            chip = origin * NY + at.y
            valid = jnp.logical_and(origin >= 0, origin < NZ)
            d = self.full(chip, self.rs.at[chip, 0], at.c, self.zs.at[chip, way], dev)

            @pl.when(valid)
            def _(d=d, nxt=nxt):
                if go and not (isinstance(k, int) and k == 0):
                    d.wait_recv()

                @pl.when(jnp.logical_and(nxt >= 0, nxt < NZ))
                def _():
                    if go:
                        d.start()
                    else:
                        d.wait_send()

    def each(self, k, f):
        at = self.at

        @pl.when(at.z - k >= 0)
        def _():
            f(at.z - k)

        @pl.when(jnp.logical_and(k > 0, at.z + k < NZ))
        def _():
            f(at.z + k)

    def ysend(self, k, go=True):
        at = self.at

        def f(zo):
            chip = zo * NY + at.y
            ways = [at.dyp, at.dym] if self.half else [at.dyp, at.dym, at.dy2]
            for i, dev in enumerate(ways):
                d = self.full(chip, self.rs.at[chip, 0], at.c, self.ys.at[chip, i], dev)
                d.start() if go else d.wait_send()
            d = self.sib(chip)
            d.start() if go else d.wait_send()

        self.each(k, f)

    def yrecv1(self, k, go=True):
        at = self.at

        def f(zo):
            for i, yo, dev in ((0, at.ym, at.dyp), (1, at.yp, at.dym)):
                chip = zo * NY + yo
                d = self.sib(chip)
                if go:
                    self.full(chip, self.rs.at[chip, 0], at.c, self.bs.at[chip], at.sib).wait_recv()
                if self.half:
                    r = self.part(chip, i, self.ys.at[chip, i], dev)
                    r.start() if go else r.wait_send()
                d.start() if go else d.wait_send()

        self.each(k, f)

    def yrecv2(self, k, go=True):
        at = self.at

        def f(zo):
            chip = zo * NY + at.y2
            d = self.sib(chip)
            if go:
                if self.half:
                    for i in (0, 1):
                        self.part(chip, i, self.bs.at[chip], at.sib).wait_recv()
                else:
                    self.full(chip, self.rs.at[chip, 0], at.c, self.bs.at[chip], at.sib).wait_recv()
                d.start()
            else:
                d.wait_send()

        self.each(k, f)

    def wait_other_core(self):
        at = self.at

        @pl.loop(0, CHIPS)
        def _(chip):
            self.full(chip, self.rb.at[chip], 1 - at.c, self.bs.at[chip], at.sib).wait_recv()


def kernel(
    q_ref, res_ref, tab_ref, bk_ref, gain_ref, k_hbm, v_hbm, wo_hbm, g_hbm, u_hbm, d_hbm,
    out_ref,
    kvb, wbuf, wob, wo_own, att_own, att_oth, res_oth,
    m_ref, l_ref, acc_ref, part_ref, rs_s, rs_r, rs2_s, rs2_r, st_ref, fin_s, fin_r, keep_ref,
    loc, kv_r, kv_b, kv_s, kv_s2, kv_bs,
    w_rs, w_rb, w_zs, w_ys, w_bs, o_rs, o_rb, o_zs, o_ys, o_bs, o_far,
    x1_s, x1_r, x2_s, x2_r, x3_s, x3_r, ca, cr, cf,
):
    at = Place()
    s, c, x, h, y, z = at.s, at.c, at.x, at.h, at.y, at.z

    loads = [
        pltpu.make_async_copy(k_hbm, kvb.at[4, c, 0], loc.at[0]),
        pltpu.make_async_copy(v_hbm, kvb.at[4, c, 1], loc.at[1]),
        pltpu.make_async_copy(g_hbm, wbuf.at[s, pl.ds(0, WROWS)], loc.at[2]),
        pltpu.make_async_copy(u_hbm, wbuf.at[s, pl.ds(WROWS, WROWS)], loc.at[3]),
        pltpu.make_async_copy(d_hbm, wbuf.at[s, pl.ds(2 * WROWS, WROWS)], loc.at[4]),
        pltpu.make_async_copy(wo_hbm, wo_own, loc.at[5]),
    ]
    for d in loads:
        d.start()

    barrier = pltpu.get_barrier_semaphore()
    peers = [at.far] + at.dx[1:] + [at.sib, at.dyp, at.dym, at.dy2]
    for dev in peers:
        pl.semaphore_signal(barrier, inc=1, device_id=dev, device_id_type=MESH)

    @pl.when(z < NZ - 1)
    def _():
        pl.semaphore_signal(barrier, inc=1, device_id=at.dzp, device_id_type=MESH)

    @pl.when(z > 0)
    def _():
        pl.semaphore_signal(barrier, inc=1, device_id=at.dzm, device_id_type=MESH)

    pl.semaphore_wait(barrier, len(peers) + (1 - (z + 1) // NZ) + (z + NZ - 1) // NZ)
    loads[0].wait()
    loads[1].wait()

    top = (y + 1) // 4
    low = 1 - (y + 3) // 4
    upper = y // 2
    lp, lm, l2 = 1 - 4 * top, 4 * low - 1, 2 - 4 * upper

    def kv_copy(o, to, send_sem, dev):
        return remote(kvb.at[o + 4, c], kvb.at[to + 4, c], send_sem, kv_r.at[to + 4], dev)

    def kv_sib(o):
        return remote(kvb.at[o + 4, c], kvb.at[o + 4, c], kv_bs.at[o + 4], kv_b.at[o + 4], at.sib)

    kz = [(kv_copy(0, -4, kv_s.at[0], at.dzp), z < NZ - 1), (kv_copy(0, 4, kv_s.at[1], at.dzm), z > 0)]
    ky = [
        kv_copy(0, -lp, kv_s.at[2], at.dyp),
        kv_copy(0, -lm, kv_s.at[3], at.dym),
        kv_copy(0, -l2, kv_s.at[4], at.dy2),
    ]
    for d, ok in kz:
        pl.when(ok)(d.start)
    for d in ky:
        d.start()
    kv_sib(0).start()

    piece = []
    for i in (0, 1):
        rows = pl.ds(pl.multiple_of(16 * (s // 4), 16), 16)
        cols = pl.ds(pl.multiple_of(1024 * i + 256 * lax.rem(s, 4), 256), 256)
        piece.append(remote(wo_hbm.at[rows, cols], wob.at[s, i], o_far.at[0, i], o_far.at[1, i], at.far))
    for d in piece:
        d.start()

    cross_r = remote(res_ref, res_oth, cr.at[0], cr.at[1], at.far)
    gw = Gather(at, wbuf, 48, w_rs, w_rb, w_zs, w_ys, w_bs)
    go = Gather(at, wob, 0, o_rs, o_rb, o_zs, o_ys, o_bs)

    for d in loads[2:5]:
        d.wait()
    gw.zstep(0)

    m_ref[...] = jnp.full(m_ref.shape, -1e30, F32)
    l_ref[...] = jnp.zeros(l_ref.shape, F32)
    acc_ref[...] = jnp.zeros(acc_ref.shape, F32)

    def update(hd, sc, v):
        m_old = m_ref[hd]
        m_new = jnp.maximum(m_old, jnp.max(sc, axis=1, keepdims=True))
        alpha = jnp.exp2(m_old - m_new)
        p = jnp.exp2(sc - m_new[:, 0:1])
        l_ref[hd] = alpha * l_ref[hd] + jnp.sum(p, axis=1, keepdims=True)
        pv = jnp.dot(p.astype(BF16), v, preferred_element_type=F32)
        acc_ref[hd] = alpha * acc_ref[hd] + pv
        m_ref[hd] = m_new

    def bias_of(hd, a, first, kt):
        idx = jnp.clip(first + kt - a + HALF_BAND // TILE, 0, OFFSETS - 1)
        return tab_ref[hd, bk_ref[a, idx]] * LOG2E

    def attend(o, core=None):
        n = 512 if core is None else 256
        first = 4 * o - 2 * c + (0 if core is None else 2 * core)
        for hd in (0, 1):
            head = slice(128 * hd, 128 * hd + 128)
            if core is None:
                k = kvb[o + 4, :, 0, :, head].reshape(n, 128)
                v = kvb[o + 4, :, 1, :, head].reshape(n, 128)
            else:
                k = kvb[o + 4, core, 0, :, head]
                v = kvb[o + 4, core, 1, :, head]
            sc = lax.dot_general(q_ref[:, head], k, (((1,), (1,)), ((), ())), preferred_element_type=F32)
            sc = jnp.concatenate(
                [
                    jnp.concatenate(
                        [
                            sc[128 * a : 128 * a + 128, 128 * kt : 128 * kt + 128] * (SCALE * LOG2E)
                            + bias_of(hd, a, first, kt)
                            for kt in range(n // 128)
                        ],
                        axis=1,
                    )
                    for a in (0, 1)
                ],
                axis=0,
            )
            if core is not None:
                row = lax.broadcasted_iota(jnp.int32, sc.shape, 0)
                col = lax.broadcasted_iota(jnp.int32, sc.shape, 1)
                dist = col - row + first * TILE
                sc = jnp.where(jnp.abs(dist) <= HALF_BAND, sc, -1e30)
            update(hd, sc, v)

    def inside(o):
        return jnp.logical_and(at.chip + o >= 0, at.chip + o < CHIPS)

    def got_own(o):
        kv_copy(o, o, kv_bs.at[0], at.sib).wait_recv()

    def got_sib(o):
        d = remote(kvb.at[o + 4, 1 - c], kvb.at[o + 4, 1 - c], kv_bs.at[o + 4], kv_b.at[o + 4], at.sib)
        d.wait_recv()

    got_sib(0)
    attend(0)

    second = []
    for i, (delta, sgn, dev) in enumerate(
        ((lp, 1 - 2 * top, at.dyp), (lm, 2 * low - 1, at.dym), (l2, 1 - 2 * upper, at.dy2))
    ):
        src = 4 * sgn
        second.append((kv_copy(src, src - delta, kv_s2.at[i], dev), inside(src)))
    for o in (-4, 4):
        pl.when(inside(o))(lambda o=o: got_own(o))
    for d, ok in second:
        pl.when(ok)(d.start)
    for o, keep in ((-4, 1), (4, 0)):
        pl.when(jnp.logical_and(inside(o), c == keep))(lambda o=o: kv_sib(o).start())
    gw.zstep(1)
    gw.ysend(0)
    for i in (0, 1):
        piece[i].wait_recv()
    go.zstep(0)
    go.ysend(0)
    cross_r.start()
    for o, core in ((-4, 0), (-4, 1), (4, 0), (4, 1)):
        need = inside(o)
        if (o, core) == (-4, 0):
            need = jnp.logical_and(need, c == 0)
        if (o, core) == (4, 1):
            need = jnp.logical_and(need, c == 1)

        @pl.when(need)
        def _(o=o, core=core):
            @pl.when(c != core)
            def _():
                got_sib(o)

            attend(o, core)

        if (o, core) == (-4, 1):
            gw.zstep(2)
            gw.ysend(1)
            go.zstep(1)
            go.ysend(1)

    wave1 = [4 * low - 1, 1 - 4 * top, 2 - 4 * upper]
    wave2 = [2 - wave1[0], -2 - wave1[1], -wave1[2]]
    for o in wave1:
        got_own(o)
        kv_sib(o).start()
    gw.zstep(3)
    gw.ysend(2)
    go.zstep(2)
    go.ysend(2)
    for n, o in enumerate(wave1):
        got_sib(o)
        attend(o)
        go.zstep(3 + n)
        go.ysend(3 + n)
        if n == 1:
            gw.zstep(4)
            gw.ysend(3)
    for o in wave2:

        @pl.when(inside(o))
        def _(o=o):
            got_own(o)
            kv_sib(o).start()

    gw.zstep(5)
    gw.ysend(4)
    go.zstep(6)
    go.ysend(6)
    for n, o in enumerate(wave2):

        @pl.when(inside(o))
        def _(o=o):
            got_sib(o)
            attend(o)

    for hd in (0, 1):
        att_own[:, 128 * hd : 128 * hd + 128] = (acc_ref[hd] / l_ref[hd]).astype(BF16)
    half = [pl.ds(0, 128), pl.ds(128, 128)]
    both = (0, 1)
    cross_a = [remote(att_own.at[half[j]], att_oth.at[half[j]], ca.at[0, j], ca.at[1, j], at.far) for j in both]
    for j in both:
        cross_a[j].start()
    gw.zstep(6)
    gw.ysend(5)
    go.zstep(7)
    go.ysend(7)
    loads[5].wait()
    order = (2, 1, 3, 0)

    def colsof(d, i):
        xd = lax.rem(x + d, NX)
        return pl.ds(pl.multiple_of(1024 * i + 256 * xd, 256), 256)

    @pl.loop(0, 4)
    def _(d):
        for i in (0, 1):
            part_ref[d, :, pl.ds(256 * i, 256)] = jnp.dot(
                att_own[...], wo_own[:, colsof(d, i)], preferred_element_type=F32
            )

    @pl.loop(0, NZ)
    def _(k):
        go.yrecv1(k)
        go.yrecv2(k)

    gw.zstep(7)
    gw.ysend(6)
    gw.ysend(7)
    go.wait_other_core()

    @pl.loop(0, 4)
    def _(k):
        gw.yrecv1(k)

    def sums(send, recv, ss, rr, j):
        return [
            remote(send.at[d - 1, half[j]], recv.at[d - 1, half[j]], ss.at[j, d - 1], rr.at[j, d - 1], at.dx[d])
            for d in (1, 2, 3)
        ]

    wob4 = wob.reshape(16, 4, 2, 16, 256)
    rs = [sums(rs_s, rs_r, x1_s, x1_r, j) for j in both]
    for j in both:
        cross_a[j].wait_recv()
        for d in order:
            xd = lax.rem(x + d, NX)
            for i in both:
                w = wob4[:, xd, i].reshape(256, 256)
                cols = pl.ds(256 * i, 256)
                p = part_ref[d, half[j], cols] + jnp.dot(att_oth[half[j], :], w, preferred_element_type=F32)
                if d:
                    rs_s[d - 1, half[j], cols] = p.astype(BF16)
                else:
                    part_ref[0, half[j], cols] = p
            if d:
                rs[j][d - 1].start()

    @pl.loop(4, NZ)
    def _(k):
        gw.yrecv1(k)

    cross_r.wait_recv()
    own = h == 0
    ag = []
    for j in both:
        for d in rs[j]:
            d.wait_recv()
        res0, res1 = res_ref[half[j], :].astype(F32), res_oth[half[j], :].astype(F32)
        for i in both:
            cols = pl.ds(256 * i, 256)
            r = jnp.where(own, res0, res1) if i == 0 else jnp.where(own, res1, res0)
            tot = part_ref[0, half[j], cols] + r
            for d in (1, 2, 3):
                tot += rs_r[d - 1, half[j], cols].astype(F32)
            st_ref[x, half[j], cols] = tot.astype(BF16)

        def slot(xo, d, j=j):
            ref = st_ref.at[xo, half[j]]
            return remote(ref, ref, x2_s.at[j, d - 1], x2_r.at[j, d - 1], at.dx[d])

        for d in (2, 1, 3):
            slot(x, d).start()
            ag.append((slot(x, d), slot(lax.rem(x + 4 - d, NX), d)))

    @pl.loop(0, NZ)
    def _(k):
        gw.yrecv2(k)

    gw.wait_other_core()

    rs2 = [sums(rs2_s, rs2_r, x3_s, x3_r, j) for j in both]
    for j in both:
        for _, d in ag[3 * j : 3 * j + 3]:
            d.wait_recv()
        ssq = jnp.zeros((128, 1), F32)
        for xo in range(NX):
            w = st_ref[xo, half[j], :].astype(F32)
            ssq += jnp.sum(w * w, axis=1, keepdims=True)
        scale = lax.rsqrt(ssq / 2048.0 + 1e-05)
        gate = jnp.zeros((128, FFB), F32)
        up = jnp.zeros((128, FFB), F32)
        for b in range(8):
            hb, xb = b // 4, b % 4
            blk = st_ref[xb, half[j], 256 * hb : 256 * hb + 256].astype(F32)
            nb = (blk * scale * gain_ref[:, 256 * b : 256 * b + 256]).astype(BF16)
            wg = wbuf[8 * b : 8 * b + 8, 0:WROWS, :].reshape(256, FFB)
            wu = wbuf[8 * b : 8 * b + 8, WROWS : 2 * WROWS, :].reshape(256, FFB)
            gate += jnp.dot(nb, wg, preferred_element_type=F32)
            up += jnp.dot(nb, wu, preferred_element_type=F32)
        hidden = (gate / (1.0 + jnp.exp(-gate)) * up).astype(BF16)
        for d in order:
            xd = lax.rem(x + d, NX)
            for i in both:
                w = wbuf[pl.ds(8 * (4 * i + xd), 8), 2 * WROWS : 3 * WROWS, :].reshape(256, FFB)
                p = lax.dot_general(hidden, w, (((1,), (1,)), ((), ())), preferred_element_type=F32)
                cols = pl.ds(256 * i, 256)
                if d:
                    rs2_s[d - 1, half[j], cols] = p.astype(BF16)
                else:
                    part_ref[0, half[j], cols] = p
            if d:
                rs2[j][d - 1].start()

    mine = pl.ds(pl.multiple_of(256 * h, 256), 256)
    theirs = pl.ds(pl.multiple_of(256 * (1 - h), 256), 256)
    cross_f = [remote(fin_s.at[half[j]], fin_r.at[half[j]], cf.at[0, j], cf.at[1, j], at.far) for j in both]

    def total(j, cols):
        tot = part_ref[0, half[j], cols]
        for d in (1, 2, 3):
            tot += rs2_r[d - 1, half[j], cols].astype(F32)
        return tot

    for j in both:
        for d in rs2[j]:
            d.wait_recv()
        fin_s[half[j], :] = total(j, theirs).astype(BF16)
        cross_f[j].start()
    for j in both:
        keep_ref[half[j], :] = total(j, mine) + st_ref[x, half[j], mine].astype(F32)

    for d, ok in kz + second:
        pl.when(ok)(d.wait_send)
    for d in ky + piece + [cross_r] + cross_a + rs[0] + rs[1] + [d for d, _ in ag] + rs2[0] + rs2[1]:
        d.wait_send()
    kv_sib(0).wait_send()
    for o in wave1:
        kv_sib(o).wait_send()
    for o in wave2:
        pl.when(inside(o))(lambda o=o: kv_sib(o).wait_send())
    for o, keep in ((-4, 1), (4, 0)):
        pl.when(jnp.logical_and(inside(o), c == keep))(lambda o=o: kv_sib(o).wait_send())

    @pl.loop(0, NZ)
    def _(k):
        for g in (gw, go):
            g.zstep(k, go=False)
            g.ysend(k, go=False)
            g.yrecv1(k, go=False)
            g.yrecv2(k, go=False)

    for j in both:
        cross_f[j].wait_recv()
        out_ref[half[j], :] = (keep_ref[half[j], :] + fin_r[half[j], :].astype(F32)).astype(BF16)
    for j in both:
        cross_f[j].wait_send()


def shards(queries, keys, values, residual_in, bias_table, buckets, out_weight, gate_weight, up_weight, down_weight_t, norm_gain):
    vmem = pl.BlockSpec(memory_space=pltpu.VMEM)
    smem = pl.BlockSpec(memory_space=pltpu.SMEM)
    hbm = pl.BlockSpec(memory_space=pl.ANY)
    dma = pltpu.SemaphoreType.DMA
    v = pltpu.VMEM
    gather_sems = [dma((CHIPS, 2)), dma((CHIPS,)), dma((CHIPS, 2)), dma((CHIPS, 3)), dma((CHIPS,))]
    scratch = [
        v((9, 2, 2, ROWS, COLS), BF16),
        v((64, 96, FFB), BF16),
        v((64, 2, 16, 256), BF16),
        v((256, 2048), BF16),
        v((ROWS, COLS), BF16),
        v((ROWS, COLS), BF16),
        v((ROWS, COLS), BF16),
        v((2, ROWS, 128), F32),
        v((2, ROWS, 128), F32),
        v((2, ROWS, 128), F32),
        v((4, ROWS, 512), F32),
        v((3, ROWS, 512), BF16),
        v((3, ROWS, 512), BF16),
        v((3, ROWS, 512), BF16),
        v((3, ROWS, 512), BF16),
        v((NX, ROWS, 512), BF16),
        v((ROWS, COLS), BF16),
        v((ROWS, COLS), BF16),
        v((ROWS, COLS), F32),
        dma((6,)), dma((9,)), dma((9,)), dma((5,)), dma((3,)), dma((9,)),
        *gather_sems,
        *gather_sems,
        dma((2, 2)),
        dma((2, 3)), dma((2, 3)), dma((2, 3)), dma((2, 3)), dma((2, 3)), dma((2, 3)),
        dma((2, 2)), dma((2,)), dma((2, 2)),
    ]
    return pl.pallas_call(
        kernel,
        out_shape=jax.ShapeDtypeStruct((ROWS, COLS), BF16),
        in_specs=[vmem, vmem, smem, smem, vmem] + [hbm] * 6,
        out_specs=vmem,
        scratch_shapes=scratch,
        compiler_params=pltpu.CompilerParams(
            collective_id=0, has_side_effects=True, vmem_limit_bytes=60 * 1024 * 1024
        ),
        name="layer",
    )(
        queries, residual_in, bias_table, buckets, norm_gain.reshape(1, -1),
        keys, values, out_weight, gate_weight, up_weight, down_weight_t,
    )


def solution(mesh):
    return jax.shard_map(
        shards,
        mesh=mesh,
        in_specs=(
            P("seq", "tp"),
            P("seq", "tp"),
            P("seq", "tp"),
            P("seq", "tp"),
            P("tp", None),
            P("seq", None),
            P("tp", None),
            P("seq", "tp"),
            P("seq", "tp"),
            P("seq", "tp"),
            P(),
        ),
        out_specs=P("seq", "tp"),
        check_vma=False,
    )
```

time: 184 us -> 131 us (0.71)
  Pallas kernels: 182 us -> 129 us
    pallas_call x1, Pallas kernels: 182 us -> 129 us  [shards(): pl.pallas_call(kernel, out_shape=jax.ShapeDtypeStruct((ROWS, COLS), BF16)...]
where the time goes in v2:
time: 131 us
  Pallas kernels  129 us (98%)
  local copies, waits for them, and re-layouts  1.57 us (1%)
    pallas_call x1, Pallas kernels, shards(): pl.pallas_call(kernel, out_shape=jax.ShapeDtypeStruct((ROWS, COLS), BF16)...  129 us

profile of v2, /device:TPU:1, one launch (start us, length us, event | category | flops | bytes accessed | tf_op | source)
XLA Modules:
  0.0 131.0 jit_solution(17155860148607563248)
XLA Ops:
  0.0 129.4 %layer.1 = bf16[256,256]{1,0:T(8,128)(2,1)} custom-call(bf16[256,256]{1,0:T(8,128)(2,1)} %q_ref.1, bf16[256,256]{1,0:T(8,128)(2,1)} %res_ref.1, f32[2,32]{1,0:T(2,128)} %tab_ref.1, s32[2,33]{1,0:T(2,128)} %bk_ref.1, f32[1,2048]{1,0:T(1,128)} %bitcast.1, bf16[256,256]{1,0:T(8,128)(2,1)} %k_hbm.1, bf16[256,256]{1,0:T(8,128)(2,1)} %v_hbm.1, ...), custom_call_target="tpu_custom_call" | custom-call | tf_op jit(solution)/shard_map/layer/pallas_call | solution.py:595
  129.5 1.6 %copy.13 = bf16[256,256]{1,0:T(8,128)(2,1)} copy(bf16[256,256]{1,0:T(8,128)(2,1)} %layer.1) | data formatting | bytes 262144

commit v3 on v2

--- a/solution.py
+++ b/solution.py
@@ -116,8 +116,7 @@
 
         def f(zo):
             chip = zo * NY + at.y
-            ways = [at.dyp, at.dym] if self.half else [at.dyp, at.dym, at.dy2]
-            for i, dev in enumerate(ways):
+            for i, dev in ((0, at.dyp), (1, at.dym)):
                 d = self.full(chip, self.rs.at[chip, 0], at.c, self.ys.at[chip, i], dev)
                 d.start() if go else d.wait_send()
             d = self.sib(chip)
@@ -134,9 +133,8 @@
                 d = self.sib(chip)
                 if go:
                     self.full(chip, self.rs.at[chip, 0], at.c, self.bs.at[chip], at.sib).wait_recv()
-                if self.half:
-                    r = self.part(chip, i, self.ys.at[chip, i], dev)
-                    r.start() if go else r.wait_send()
+                r = self.part(chip, i, self.ys.at[chip, i], dev)
+                r.start() if go else r.wait_send()
                 d.start() if go else d.wait_send()
 
         self.each(k, f)
@@ -148,11 +146,8 @@
             chip = zo * NY + at.y2
             d = self.sib(chip)
             if go:
-                if self.half:
-                    for i in (0, 1):
-                        self.part(chip, i, self.bs.at[chip], at.sib).wait_recv()
-                else:
-                    self.full(chip, self.rs.at[chip, 0], at.c, self.bs.at[chip], at.sib).wait_recv()
+                for i in (0, 1):
+                    self.part(chip, i, self.bs.at[chip], at.sib).wait_recv()
                 d.start()
             else:
                 d.wait_send()
@@ -165,13 +160,66 @@
         @pl.loop(0, CHIPS)
         def _(chip):
             self.full(chip, self.rb.at[chip], 1 - at.c, self.bs.at[chip], at.sib).wait_recv()
+
+
+class Pieces:
+    def __init__(self, at, buf, rs, rb, zs, ys, bs):
+        self.at, self.buf = at, buf
+        self.rs, self.rb, self.zs, self.ys, self.bs = rs, rb, zs, ys, bs
+        self.q = lax.rem(at.z, 4)
+        self.base = at.z - self.q
+
+    def copy(self, chip, core, send_sem, recv_sem, dev):
+        slot = self.buf.at[chip * 2 + core]
+        return remote(slot, slot, send_sem, recv_sem.at[chip], dev)
+
+    def wait(self, chip):
+        self.copy(chip, self.at.c, self.bs.at[chip], self.rs, self.at.sib).wait_recv()
+
+    def sib(self, chip):
+        return self.copy(chip, self.at.c, self.bs.at[chip], self.rb, self.at.sib)
+
+    def zsend(self, go=True):
+        at = self.at
+        for d in (1, 3, 2):
+            dev = at.dev(self.base + lax.rem(self.q + d, 4), at.y)
+            r = self.copy(self.q * NY + at.y, at.c, self.zs.at[d - 1], self.rs, dev)
+            r.start() if go else r.wait_send()
+
+    def ysend(self, go=True):
+        at = self.at
+        for d in range(4):
+            chip = lax.rem(self.q + d, 4) * NY + at.y
+            if go and d:
+                self.wait(chip)
+            for i, dev in enumerate((at.dyp, at.dym, at.dy2)):
+                r = self.copy(chip, at.c, self.ys.at[d, i], self.rs, dev)
+                r.start() if go else r.wait_send()
+            r = self.sib(chip)
+            r.start() if go else r.wait_send()
+
+    def yrecv(self, go=True):
+        at = self.at
+        for d in range(4):
+            for yo in (at.yp, at.ym, at.y2):
+                chip = lax.rem(self.q + d, 4) * NY + yo
+                r = self.sib(chip)
+                if go:
+                    self.wait(chip)
+                    r.start()
+                else:
+                    r.wait_send()
+
+    def wait_other_core(self):
+        for chip in range(16):
+            self.copy(chip, 1 - self.at.c, self.bs.at[chip], self.rb, self.at.sib).wait_recv()
 
 
 def kernel(
     q_ref, res_ref, tab_ref, bk_ref, gain_ref, k_hbm, v_hbm, wo_hbm, g_hbm, u_hbm, d_hbm,
     out_ref,
     kvb, wbuf, wob, wo_own, att_own, att_oth, res_oth,
-    m_ref, l_ref, acc_ref, part_ref, rs_s, rs_r, rs2_s, rs2_r, st_ref, fin_s, fin_r, keep_ref,
+    m_ref, l_ref, acc_ref, part_ref, rs_s, rs_r, rs2_s, rs2_r, st_ref, fin_s, fin_r, keep_ref, hid_ref,
     loc, kv_r, kv_b, kv_s, kv_s2, kv_bs,
     w_rs, w_rb, w_zs, w_ys, w_bs, o_rs, o_rb, o_zs, o_ys, o_bs, o_far,
     x1_s, x1_r, x2_s, x2_r, x3_s, x3_r, ca, cr, cf,
@@ -191,19 +239,23 @@
         d.start()
 
     barrier = pltpu.get_barrier_semaphore()
-    peers = [at.far] + at.dx[1:] + [at.sib, at.dyp, at.dym, at.dy2]
+    quad = [at.dev(z - lax.rem(z, 4) + lax.rem(z + d, 4), y) for d in (1, 2, 3)]
+    peers = [at.far] + at.dx[1:] + quad + [at.sib, at.dyp, at.dym, at.dy2]
     for dev in peers:
         pl.semaphore_signal(barrier, inc=1, device_id=dev, device_id_type=MESH)
 
-    @pl.when(z < NZ - 1)
+    @pl.when(z == 3)
     def _():
         pl.semaphore_signal(barrier, inc=1, device_id=at.dzp, device_id_type=MESH)
 
-    @pl.when(z > 0)
+    @pl.when(z == 4)
     def _():
         pl.semaphore_signal(barrier, inc=1, device_id=at.dzm, device_id_type=MESH)
 
-    pl.semaphore_wait(barrier, len(peers) + (1 - (z + 1) // NZ) + (z + NZ - 1) // NZ)
+    m_ref[...] = jnp.full(m_ref.shape, -1e30, F32)
+    l_ref[...] = jnp.zeros(l_ref.shape, F32)
+    acc_ref[...] = jnp.zeros(acc_ref.shape, F32)
+    pl.semaphore_wait(barrier, len(peers) + (z + 1) // 4 - z // 5 - z // 7)
     loads[0].wait()
     loads[1].wait()
 
@@ -220,35 +272,31 @@
 
     kz = [(kv_copy(0, -4, kv_s.at[0], at.dzp), z < NZ - 1), (kv_copy(0, 4, kv_s.at[1], at.dzm), z > 0)]
     ky = [
+        kv_copy(0, -l2, kv_s.at[4], at.dy2),
         kv_copy(0, -lp, kv_s.at[2], at.dyp),
         kv_copy(0, -lm, kv_s.at[3], at.dym),
-        kv_copy(0, -l2, kv_s.at[4], at.dy2),
     ]
+    piece = []
+    slot = (lax.rem(z, 4) * NY + y) * 2 + c
+    for i in (0, 1):
+        rows = pl.ds(pl.multiple_of(32 * (slot // 4), 32), 32)
+        cols = pl.ds(pl.multiple_of(1024 * i + 256 * lax.rem(slot, 4), 256), 256)
+        piece.append(remote(wo_hbm.at[rows, cols], wob.at[slot, i], o_far.at[0, i], o_far.at[1, i], at.far))
+    for d in piece:
+        d.start()
     for d, ok in kz:
         pl.when(ok)(d.start)
     for d in ky:
         d.start()
     kv_sib(0).start()
 
-    piece = []
-    for i in (0, 1):
-        rows = pl.ds(pl.multiple_of(16 * (s // 4), 16), 16)
-        cols = pl.ds(pl.multiple_of(1024 * i + 256 * lax.rem(s, 4), 256), 256)
-        piece.append(remote(wo_hbm.at[rows, cols], wob.at[s, i], o_far.at[0, i], o_far.at[1, i], at.far))
-    for d in piece:
-        d.start()
-
     cross_r = remote(res_ref, res_oth, cr.at[0], cr.at[1], at.far)
     gw = Gather(at, wbuf, 48, w_rs, w_rb, w_zs, w_ys, w_bs)
-    go = Gather(at, wob, 0, o_rs, o_rb, o_zs, o_ys, o_bs)
+    go = Pieces(at, wob, o_rs, o_rb, o_zs, o_ys, o_bs)
 
     for d in loads[2:5]:
         d.wait()
     gw.zstep(0)
-
-    m_ref[...] = jnp.full(m_ref.shape, -1e30, F32)
-    l_ref[...] = jnp.zeros(l_ref.shape, F32)
-    acc_ref[...] = jnp.zeros(acc_ref.shape, F32)
 
     def update(hd, sc, v):
         m_old = m_ref[hd]
@@ -311,24 +359,28 @@
     attend(0)
 
     second = []
-    for i, (delta, sgn, dev) in enumerate(
-        ((lp, 1 - 2 * top, at.dyp), (lm, 2 * low - 1, at.dym), (l2, 1 - 2 * upper, at.dy2))
-    ):
+    for i, (delta, sgn, dev) in enumerate(((lp, 1 - 2 * top, at.dyp), (lm, 2 * low - 1, at.dym))):
         src = 4 * sgn
         second.append((kv_copy(src, src - delta, kv_s2.at[i], dev), inside(src)))
+    near = [2 - 4 * upper, 4 * low - 1, 1 - 4 * top]
+    last = [2 - near[1], -2 - near[2], -near[0]]
+    zt = z + 1 - 2 * upper
+    across = (kv_copy(near[0], -near[0], kv_s2.at[2], at.dev(zt, y)), jnp.logical_and(zt >= 0, zt < NZ))
     for o in (-4, 4):
         pl.when(inside(o))(lambda o=o: got_own(o))
     for d, ok in second:
         pl.when(ok)(d.start)
     for o, keep in ((-4, 1), (4, 0)):
         pl.when(jnp.logical_and(inside(o), c == keep))(lambda o=o: kv_sib(o).start())
+    got_own(near[0])
+    pl.when(across[1])(across[0].start)
+    kv_sib(near[0]).start()
+    second.append(across)
+    for i in (0, 1):
+        piece[i].wait_recv()
+    go.zsend()
     gw.zstep(1)
     gw.ysend(0)
-    for i in (0, 1):
-        piece[i].wait_recv()
-    go.zstep(0)
-    go.ysend(0)
-    cross_r.start()
     for o, core in ((-4, 0), (-4, 1), (4, 0), (4, 1)):
         need = inside(o)
         if (o, core) == (-4, 0):
@@ -345,29 +397,24 @@
             attend(o, core)
 
         if (o, core) == (-4, 1):
+            for near_o in near[1:]:
+                got_own(near_o)
+                kv_sib(near_o).start()
             gw.zstep(2)
-            gw.ysend(1)
-            go.zstep(1)
-            go.ysend(1)
-
-    wave1 = [4 * low - 1, 1 - 4 * top, 2 - 4 * upper]
-    wave2 = [2 - wave1[0], -2 - wave1[1], -wave1[2]]
-    for o in wave1:
-        got_own(o)
-        kv_sib(o).start()
-    gw.zstep(3)
-    gw.ysend(2)
-    go.zstep(2)
-    go.ysend(2)
-    for n, o in enumerate(wave1):
+            go.ysend()
+            cross_r.start()
+
+    gw.ysend(1)
+    for n, o in enumerate(near):
         got_sib(o)
         attend(o)
-        go.zstep(3 + n)
-        go.ysend(3 + n)
-        if n == 1:
+        if n == 0:
+            gw.zstep(3)
+            gw.ysend(2)
+        if n == 2:
             gw.zstep(4)
             gw.ysend(3)
-    for o in wave2:
+    for o in last:
 
         @pl.when(inside(o))
         def _(o=o):
@@ -376,9 +423,7 @@
 
     gw.zstep(5)
     gw.ysend(4)
-    go.zstep(6)
-    go.ysend(6)
-    for n, o in enumerate(wave2):
+    for n, o in enumerate(last):
 
         @pl.when(inside(o))
         def _(o=o):
@@ -392,10 +437,9 @@
     cross_a = [remote(att_own.at[half[j]], att_oth.at[half[j]], ca.at[0, j], ca.at[1, j], at.far) for j in both]
     for j in both:
         cross_a[j].start()
+    go.yrecv()
     gw.zstep(6)
     gw.ysend(5)
-    go.zstep(7)
-    go.ysend(7)
     loads[5].wait()
     order = (2, 1, 3, 0)
 
@@ -410,11 +454,6 @@
                 att_own[...], wo_own[:, colsof(d, i)], preferred_element_type=F32
             )
 
-    @pl.loop(0, NZ)
-    def _(k):
-        go.yrecv1(k)
-        go.yrecv2(k)
-
     gw.zstep(7)
     gw.ysend(6)
     gw.ysend(7)
@@ -430,7 +469,7 @@
             for d in (1, 2, 3)
         ]
 
-    wob4 = wob.reshape(16, 4, 2, 16, 256)
+    wob4 = wob.reshape(8, 4, 2, 32, 256)
     rs = [sums(rs_s, rs_r, x1_s, x1_r, j) for j in both]
     for j in both:
         cross_a[j].wait_recv()
@@ -480,7 +519,42 @@
 
     gw.wait_other_core()
 
-    rs2 = [sums(rs2_s, rs2_r, x3_s, x3_r, j) for j in both]
+    def sums2(kind, j):
+        return [
+            remote(
+                rs2_s.at[kind, d - 1, half[j]], rs2_r.at[kind, d - 1, half[j]],
+                x3_s.at[kind, j, d - 1], x3_r.at[kind, j, d - 1], at.dx[d],
+            )
+            for d in (1, 2, 3)
+        ]
+
+    rs2 = [[sums2(kind, j) for j in both] for kind in both]
+    cross_f = [remote(fin_s.at[half[j]], fin_r.at[half[j]], cf.at[0, j], cf.at[1, j], at.far) for j in both]
+
+    def down(kind, j):
+        cols = 1 - h if kind == 0 else h
+        for d in order:
+            xd = lax.rem(x + d, NX)
+            w = wbuf[pl.ds(8 * (4 * cols + xd), 8), 2 * WROWS : 3 * WROWS, :].reshape(256, FFB)
+            p = lax.dot_general(hid_ref[half[j], :], w, (((1,), (1,)), ((), ())), preferred_element_type=F32)
+            if d:
+                rs2_s[kind, d - 1, half[j], :] = p.astype(BF16)
+                rs2[kind][j][d - 1].start()
+            else:
+                keep_ref[kind, half[j], :] = p
+
+    def total(kind, j):
+        for d in rs2[kind][j]:
+            d.wait_recv()
+        tot = keep_ref[kind, half[j], :]
+        for d in (1, 2, 3):
+            tot += rs2_r[kind, d - 1, half[j], :].astype(F32)
+        return tot
+
+    def cross(j):
+        fin_s[half[j], :] = total(0, j).astype(BF16)
+        cross_f[j].start()
+
     for j in both:
         for _, d in ag[3 * j : 3 * j + 3]:
             d.wait_recv()
@@ -499,61 +573,43 @@
             wu = wbuf[8 * b : 8 * b + 8, WROWS : 2 * WROWS, :].reshape(256, FFB)
             gate += jnp.dot(nb, wg, preferred_element_type=F32)
             up += jnp.dot(nb, wu, preferred_element_type=F32)
-        hidden = (gate / (1.0 + jnp.exp(-gate)) * up).astype(BF16)
-        for d in order:
-            xd = lax.rem(x + d, NX)
-            for i in both:
-                w = wbuf[pl.ds(8 * (4 * i + xd), 8), 2 * WROWS : 3 * WROWS, :].reshape(256, FFB)
-                p = lax.dot_general(hidden, w, (((1,), (1,)), ((), ())), preferred_element_type=F32)
-                cols = pl.ds(256 * i, 256)
-                if d:
-                    rs2_s[d - 1, half[j], cols] = p.astype(BF16)
-                else:
-                    part_ref[0, half[j], cols] = p
-            if d:
-                rs2[j][d - 1].start()
-
+        hid_ref[half[j], :] = (gate / (1.0 + jnp.exp(-gate)) * up).astype(BF16)
+        if j:
+            cross(0)
+        down(0, j)
+
+    down(1, 0)
+    cross(1)
+    down(1, 1)
     mine = pl.ds(pl.multiple_of(256 * h, 256), 256)
-    theirs = pl.ds(pl.multiple_of(256 * (1 - h), 256), 256)
-    cross_f = [remote(fin_s.at[half[j]], fin_r.at[half[j]], cf.at[0, j], cf.at[1, j], at.far) for j in both]
-
-    def total(j, cols):
-        tot = part_ref[0, half[j], cols]
-        for d in (1, 2, 3):
-            tot += rs2_r[d - 1, half[j], cols].astype(F32)
-        return tot
-
     for j in both:
-        for d in rs2[j]:
-            d.wait_recv()
-        fin_s[half[j], :] = total(j, theirs).astype(BF16)
-        cross_f[j].start()
-    for j in both:
-        keep_ref[half[j], :] = total(j, mine) + st_ref[x, half[j], mine].astype(F32)
+        keep_ref[1, half[j], :] = total(1, j) + st_ref[x, half[j], mine].astype(F32)
 
     for d, ok in kz + second:
         pl.when(ok)(d.wait_send)
-    for d in ky + piece + [cross_r] + cross_a + rs[0] + rs[1] + [d for d, _ in ag] + rs2[0] + rs2[1]:
+    for d in ky + piece + [cross_r] + cross_a + rs[0] + rs[1] + [d for d, _ in ag] + sum(rs2[0] + rs2[1], []):
         d.wait_send()
     kv_sib(0).wait_send()
-    for o in wave1:
+    for o in near:
         kv_sib(o).wait_send()
-    for o in wave2:
+    for o in last:
         pl.when(inside(o))(lambda o=o: kv_sib(o).wait_send())
     for o, keep in ((-4, 1), (4, 0)):
         pl.when(jnp.logical_and(inside(o), c == keep))(lambda o=o: kv_sib(o).wait_send())
 
     @pl.loop(0, NZ)
     def _(k):
-        for g in (gw, go):
-            g.zstep(k, go=False)
-            g.ysend(k, go=False)
-            g.yrecv1(k, go=False)
-            g.yrecv2(k, go=False)
-
+        gw.zstep(k, go=False)
+        gw.ysend(k, go=False)
+        gw.yrecv1(k, go=False)
+        gw.yrecv2(k, go=False)
+
+    go.zsend(go=False)
+    go.ysend(go=False)
+    go.yrecv(go=False)
     for j in both:
         cross_f[j].wait_recv()
-        out_ref[half[j], :] = (keep_ref[half[j], :] + fin_r[half[j], :].astype(F32)).astype(BF16)
+        out_ref[half[j], :] = (keep_ref[1, half[j], :] + fin_r[half[j], :].astype(F32)).astype(BF16)
     for j in both:
         cross_f[j].wait_send()
 
@@ -564,11 +620,11 @@
     hbm = pl.BlockSpec(memory_space=pl.ANY)
     dma = pltpu.SemaphoreType.DMA
     v = pltpu.VMEM
-    gather_sems = [dma((CHIPS, 2)), dma((CHIPS,)), dma((CHIPS, 2)), dma((CHIPS, 3)), dma((CHIPS,))]
+    gather_sems = [dma((CHIPS, 2)), dma((CHIPS,)), dma((CHIPS, 2)), dma((CHIPS, 2)), dma((CHIPS,))]
     scratch = [
         v((9, 2, 2, ROWS, COLS), BF16),
         v((64, 96, FFB), BF16),
-        v((64, 2, 16, 256), BF16),
+        v((32, 2, 32, 256), BF16),
         v((256, 2048), BF16),
         v((ROWS, COLS), BF16),
         v((ROWS, COLS), BF16),
@@ -579,17 +635,18 @@
         v((4, ROWS, 512), F32),
         v((3, ROWS, 512), BF16),
         v((3, ROWS, 512), BF16),
-        v((3, ROWS, 512), BF16),
-        v((3, ROWS, 512), BF16),
+        v((2, 3, ROWS, COLS), BF16),
+        v((2, 3, ROWS, COLS), BF16),
         v((NX, ROWS, 512), BF16),
         v((ROWS, COLS), BF16),
         v((ROWS, COLS), BF16),
-        v((ROWS, COLS), F32),
+        v((2, ROWS, COLS), F32),
+        v((ROWS, FFB), BF16),
         dma((6,)), dma((9,)), dma((9,)), dma((5,)), dma((3,)), dma((9,)),
         *gather_sems,
-        *gather_sems,
+        dma((16,)), dma((16,)), dma((3,)), dma((4, 3)), dma((16,)),
         dma((2, 2)),
-        dma((2, 3)), dma((2, 3)), dma((2, 3)), dma((2, 3)), dma((2, 3)), dma((2, 3)),
+        dma((2, 3)), dma((2, 3)), dma((2, 3)), dma((2, 3)), dma((2, 2, 3)), dma((2, 2, 3)),
         dma((2, 2)), dma((2,)), dma((2, 2)),
     ]
     return pl.pallas_call(

time: 131 us -> 123 us (0.939)
  the two profiles are of different devices: /device:TPU:1 before, /device:TPU:56 now
where the time goes in v3:
time: 123 us
  Pallas kernels  122 us (99%)
  local copies, waits for them, and re-layouts  1.57 us (1%)
    pallas_call x1, Pallas kernels, shards(): pl.pallas_call(kernel, out_shape=jax.ShapeDtypeStruct((ROWS, COLS), BF16)...  122 us

profile of v3, /device:TPU:56, one launch (start us, length us, event | category | flops | bytes accessed | tf_op | source)
XLA Modules:
  0.0 123.3 jit_solution(7851706074242779739)
XLA Ops:
  0.0 121.7 %layer.1 = bf16[256,256]{1,0:T(8,128)(2,1)} custom-call(bf16[256,256]{1,0:T(8,128)(2,1)} %q_ref.1, bf16[256,256]{1,0:T(8,128)(2,1)} %res_ref.1, f32[2,32]{1,0:T(2,128)} %tab_ref.1, s32[2,33]{1,0:T(2,128)} %bk_ref.1, f32[1,2048]{1,0:T(1,128)} %bitcast.1, bf16[256,256]{1,0:T(8,128)(2,1)} %k_hbm.1, bf16[256,256]{1,0:T(8,128)(2,1)} %v_hbm.1, ...), custom_call_target="tpu_custom_call" | custom-call | tf_op jit(solution)/shard_map/layer/pallas_call | solution.py:652
  121.7 1.6 %copy.13 = bf16[256,256]{1,0:T(8,128)(2,1)} copy(bf16[256,256]{1,0:T(8,128)(2,1)} %layer.1) | data formatting | bytes 262144

commit v4 on v3

--- a/solution.py
+++ b/solution.py
@@ -162,67 +162,14 @@
             self.full(chip, self.rb.at[chip], 1 - at.c, self.bs.at[chip], at.sib).wait_recv()
 
 
-class Pieces:
-    def __init__(self, at, buf, rs, rb, zs, ys, bs):
-        self.at, self.buf = at, buf
-        self.rs, self.rb, self.zs, self.ys, self.bs = rs, rb, zs, ys, bs
-        self.q = lax.rem(at.z, 4)
-        self.base = at.z - self.q
-
-    def copy(self, chip, core, send_sem, recv_sem, dev):
-        slot = self.buf.at[chip * 2 + core]
-        return remote(slot, slot, send_sem, recv_sem.at[chip], dev)
-
-    def wait(self, chip):
-        self.copy(chip, self.at.c, self.bs.at[chip], self.rs, self.at.sib).wait_recv()
-
-    def sib(self, chip):
-        return self.copy(chip, self.at.c, self.bs.at[chip], self.rb, self.at.sib)
-
-    def zsend(self, go=True):
-        at = self.at
-        for d in (1, 3, 2):
-            dev = at.dev(self.base + lax.rem(self.q + d, 4), at.y)
-            r = self.copy(self.q * NY + at.y, at.c, self.zs.at[d - 1], self.rs, dev)
-            r.start() if go else r.wait_send()
-
-    def ysend(self, go=True):
-        at = self.at
-        for d in range(4):
-            chip = lax.rem(self.q + d, 4) * NY + at.y
-            if go and d:
-                self.wait(chip)
-            for i, dev in enumerate((at.dyp, at.dym, at.dy2)):
-                r = self.copy(chip, at.c, self.ys.at[d, i], self.rs, dev)
-                r.start() if go else r.wait_send()
-            r = self.sib(chip)
-            r.start() if go else r.wait_send()
-
-    def yrecv(self, go=True):
-        at = self.at
-        for d in range(4):
-            for yo in (at.yp, at.ym, at.y2):
-                chip = lax.rem(self.q + d, 4) * NY + yo
-                r = self.sib(chip)
-                if go:
-                    self.wait(chip)
-                    r.start()
-                else:
-                    r.wait_send()
-
-    def wait_other_core(self):
-        for chip in range(16):
-            self.copy(chip, 1 - self.at.c, self.bs.at[chip], self.rb, self.at.sib).wait_recv()
-
-
 def kernel(
     q_ref, res_ref, tab_ref, bk_ref, gain_ref, k_hbm, v_hbm, wo_hbm, g_hbm, u_hbm, d_hbm,
     out_ref,
-    kvb, wbuf, wob, wo_own, att_own, att_oth, res_oth,
+    kvb, wbuf, wo_own, att_own, mid_s, mid_r,
     m_ref, l_ref, acc_ref, part_ref, rs_s, rs_r, rs2_s, rs2_r, st_ref, fin_s, fin_r, keep_ref, hid_ref,
     loc, kv_r, kv_b, kv_s, kv_s2, kv_bs,
-    w_rs, w_rb, w_zs, w_ys, w_bs, o_rs, o_rb, o_zs, o_ys, o_bs, o_far,
-    x1_s, x1_r, x2_s, x2_r, x3_s, x3_r, ca, cr, cf,
+    w_rs, w_rb, w_zs, w_ys, w_bs,
+    x1_s, x1_r, x2_s, x2_r, x3_s, x3_r, ca, cf,
 ):
     at = Place()
     s, c, x, h, y, z = at.s, at.c, at.x, at.h, at.y, at.z
@@ -239,23 +186,22 @@
         d.start()
 
     barrier = pltpu.get_barrier_semaphore()
-    quad = [at.dev(z - lax.rem(z, 4) + lax.rem(z + d, 4), y) for d in (1, 2, 3)]
-    peers = [at.far] + at.dx[1:] + quad + [at.sib, at.dyp, at.dym, at.dy2]
+    peers = [at.far] + at.dx[1:] + [at.sib, at.dyp, at.dym, at.dy2]
     for dev in peers:
         pl.semaphore_signal(barrier, inc=1, device_id=dev, device_id_type=MESH)
 
-    @pl.when(z == 3)
+    @pl.when(z < NZ - 1)
     def _():
         pl.semaphore_signal(barrier, inc=1, device_id=at.dzp, device_id_type=MESH)
 
-    @pl.when(z == 4)
+    @pl.when(z > 0)
     def _():
         pl.semaphore_signal(barrier, inc=1, device_id=at.dzm, device_id_type=MESH)
 
     m_ref[...] = jnp.full(m_ref.shape, -1e30, F32)
     l_ref[...] = jnp.zeros(l_ref.shape, F32)
     acc_ref[...] = jnp.zeros(acc_ref.shape, F32)
-    pl.semaphore_wait(barrier, len(peers) + (z + 1) // 4 - z // 5 - z // 7)
+    pl.semaphore_wait(barrier, len(peers) + (1 - (z + 1) // NZ) + (z + NZ - 1) // NZ)
     loads[0].wait()
     loads[1].wait()
 
@@ -276,23 +222,13 @@
         kv_copy(0, -lp, kv_s.at[2], at.dyp),
         kv_copy(0, -lm, kv_s.at[3], at.dym),
     ]
-    piece = []
-    slot = (lax.rem(z, 4) * NY + y) * 2 + c
-    for i in (0, 1):
-        rows = pl.ds(pl.multiple_of(32 * (slot // 4), 32), 32)
-        cols = pl.ds(pl.multiple_of(1024 * i + 256 * lax.rem(slot, 4), 256), 256)
-        piece.append(remote(wo_hbm.at[rows, cols], wob.at[slot, i], o_far.at[0, i], o_far.at[1, i], at.far))
-    for d in piece:
-        d.start()
     for d, ok in kz:
         pl.when(ok)(d.start)
     for d in ky:
         d.start()
     kv_sib(0).start()
 
-    cross_r = remote(res_ref, res_oth, cr.at[0], cr.at[1], at.far)
     gw = Gather(at, wbuf, 48, w_rs, w_rb, w_zs, w_ys, w_bs)
-    go = Pieces(at, wob, o_rs, o_rb, o_zs, o_ys, o_bs)
 
     for d in loads[2:5]:
         d.wait()
@@ -376,9 +312,6 @@
     pl.when(across[1])(across[0].start)
     kv_sib(near[0]).start()
     second.append(across)
-    for i in (0, 1):
-        piece[i].wait_recv()
-    go.zsend()
     gw.zstep(1)
     gw.ysend(0)
     for o, core in ((-4, 0), (-4, 1), (4, 0), (4, 1)):
@@ -401,19 +334,13 @@
                 got_own(near_o)
                 kv_sib(near_o).start()
             gw.zstep(2)
-            go.ysend()
-            cross_r.start()
 
     gw.ysend(1)
     for n, o in enumerate(near):
         got_sib(o)
         attend(o)
-        if n == 0:
-            gw.zstep(3)
-            gw.ysend(2)
-        if n == 2:
-            gw.zstep(4)
-            gw.ysend(3)
+        gw.zstep(3 + n)
+        gw.ysend(2 + n)
     for o in last:
 
         @pl.when(inside(o))
@@ -421,8 +348,8 @@
             got_own(o)
             kv_sib(o).start()
 
-    gw.zstep(5)
-    gw.ysend(4)
+    gw.zstep(6)
+    gw.ysend(5)
     for n, o in enumerate(last):
 
         @pl.when(inside(o))
@@ -430,92 +357,74 @@
             got_sib(o)
             attend(o)
 
+        if n == 0:
+            gw.zstep(7)
+            gw.ysend(6)
+            gw.ysend(7)
+
     for hd in (0, 1):
         att_own[:, 128 * hd : 128 * hd + 128] = (acc_ref[hd] / l_ref[hd]).astype(BF16)
     half = [pl.ds(0, 128), pl.ds(128, 128)]
     both = (0, 1)
-    cross_a = [remote(att_own.at[half[j]], att_oth.at[half[j]], ca.at[0, j], ca.at[1, j], at.far) for j in both]
-    for j in both:
-        cross_a[j].start()
-    go.yrecv()
-    gw.zstep(6)
-    gw.ysend(5)
+    quart = [pl.ds(64 * j, 64) for j in range(4)]
     loads[5].wait()
     order = (2, 1, 3, 0)
 
-    def colsof(d, i):
-        xd = lax.rem(x + d, NX)
-        return pl.ds(pl.multiple_of(1024 * i + 256 * xd, 256), 256)
-
-    @pl.loop(0, 4)
-    def _(d):
-        for i in (0, 1):
-            part_ref[d, :, pl.ds(256 * i, 256)] = jnp.dot(
-                att_own[...], wo_own[:, colsof(d, i)], preferred_element_type=F32
-            )
-
-    gw.zstep(7)
-    gw.ysend(6)
-    gw.ysend(7)
-    go.wait_other_core()
-
-    @pl.loop(0, 4)
-    def _(k):
-        gw.yrecv1(k)
-
-    def sums(send, recv, ss, rr, j):
-        return [
-            remote(send.at[d - 1, half[j]], recv.at[d - 1, half[j]], ss.at[j, d - 1], rr.at[j, d - 1], at.dx[d])
+    rs = [
+        [
+            remote(rs_s.at[d - 1, q], rs_r.at[d - 1, q], x1_s.at[j, d - 1], x1_r.at[j, d - 1], at.dx[d])
             for d in (1, 2, 3)
         ]
-
-    wob4 = wob.reshape(8, 4, 2, 32, 256)
-    rs = [sums(rs_s, rs_r, x1_s, x1_r, j) for j in both]
+        for j, q in enumerate(quart)
+    ]
     for j in both:
-        cross_a[j].wait_recv()
         for d in order:
-            xd = lax.rem(x + d, NX)
             for i in both:
-                w = wob4[:, xd, i].reshape(256, 256)
+                w = wo_own[:, pl.ds(pl.multiple_of(1024 * i + 256 * lax.rem(x + d, NX), 256), 256)]
+                p = jnp.dot(att_own[half[j], :], w, preferred_element_type=F32)
                 cols = pl.ds(256 * i, 256)
-                p = part_ref[d, half[j], cols] + jnp.dot(att_oth[half[j], :], w, preferred_element_type=F32)
                 if d:
                     rs_s[d - 1, half[j], cols] = p.astype(BF16)
                 else:
-                    part_ref[0, half[j], cols] = p
+                    part_ref[half[j], cols] = p
             if d:
-                rs[j][d - 1].start()
-
-    @pl.loop(4, NZ)
+                rs[2 * j][d - 1].start()
+        for d in (2, 1, 3):
+            rs[2 * j + 1][d - 1].start()
+
+    cross_a = [remote(mid_s.at[q], mid_r.at[q], ca.at[0, j], ca.at[1, j], at.far) for j, q in enumerate(quart)]
+    for j, q in enumerate(quart):
+        for d in rs[j]:
+            d.wait_recv()
+        res = res_ref[q, :].astype(F32)
+        for i in both:
+            cols = pl.ds(256 * i, 256)
+            tot = part_ref[q, cols] + jnp.where(h == i, res, 0.0)
+            for d in (1, 2, 3):
+                tot += rs_r[d - 1, q, cols].astype(F32)
+            mid_s[q, cols] = tot.astype(BF16)
+        cross_a[j].start()
+
+    @pl.loop(0, NZ)
     def _(k):
         gw.yrecv1(k)
-
-    cross_r.wait_recv()
-    own = h == 0
-    ag = []
-    for j in both:
-        for d in rs[j]:
-            d.wait_recv()
-        res0, res1 = res_ref[half[j], :].astype(F32), res_oth[half[j], :].astype(F32)
-        for i in both:
-            cols = pl.ds(256 * i, 256)
-            r = jnp.where(own, res0, res1) if i == 0 else jnp.where(own, res1, res0)
-            tot = part_ref[0, half[j], cols] + r
-            for d in (1, 2, 3):
-                tot += rs_r[d - 1, half[j], cols].astype(F32)
-            st_ref[x, half[j], cols] = tot.astype(BF16)
-
-        def slot(xo, d, j=j):
-            ref = st_ref.at[xo, half[j]]
-            return remote(ref, ref, x2_s.at[j, d - 1], x2_r.at[j, d - 1], at.dx[d])
-
-        for d in (2, 1, 3):
-            slot(x, d).start()
-            ag.append((slot(x, d), slot(lax.rem(x + 4 - d, NX), d)))
 
     @pl.loop(0, NZ)
     def _(k):
         gw.yrecv2(k)
+
+    ag = []
+    for j, q in enumerate(quart):
+        cross_a[j].wait_recv()
+        st_ref[x, q, :] = (mid_s[q, :].astype(F32) + mid_r[q, :].astype(F32)).astype(BF16)
+
+        def share(xo, d, j=j, q=q):
+            ref = st_ref.at[xo, q]
+            return remote(ref, ref, x2_s.at[j, d - 1], x2_r.at[j, d - 1], at.dx[d])
+
+        for d in (2, 1, 3):
+            share(x, d).start()
+            ag.append((share(x, d), share(lax.rem(x + 4 - d, NX), d)))
 
     gw.wait_other_core()
 
@@ -556,7 +465,7 @@
         cross_f[j].start()
 
     for j in both:
-        for _, d in ag[3 * j : 3 * j + 3]:
+        for _, d in ag[6 * j : 6 * j + 6]:
             d.wait_recv()
         ssq = jnp.zeros((128, 1), F32)
         for xo in range(NX):
@@ -587,7 +496,7 @@
 
     for d, ok in kz + second:
         pl.when(ok)(d.wait_send)
-    for d in ky + piece + [cross_r] + cross_a + rs[0] + rs[1] + [d for d, _ in ag] + sum(rs2[0] + rs2[1], []):
+    for d in ky + cross_a + sum(rs, []) + [d for d, _ in ag] + sum(rs2[0] + rs2[1], []):
         d.wait_send()
     kv_sib(0).wait_send()
     for o in near:
@@ -604,9 +513,6 @@
         gw.yrecv1(k, go=False)
         gw.yrecv2(k, go=False)
 
-    go.zsend(go=False)
-    go.ysend(go=False)
-    go.yrecv(go=False)
     for j in both:
         cross_f[j].wait_recv()
         out_ref[half[j], :] = (keep_ref[1, half[j], :] + fin_r[half[j], :].astype(F32)).astype(BF16)
@@ -624,15 +530,14 @@
     scratch = [
         v((9, 2, 2, ROWS, COLS), BF16),
         v((64, 96, FFB), BF16),
-        v((32, 2, 32, 256), BF16),
         v((256, 2048), BF16),
         v((ROWS, COLS), BF16),
-        v((ROWS, COLS), BF16),
-        v((ROWS, COLS), BF16),
+        v((ROWS, 512), BF16),
+        v((ROWS, 512), BF16),
         v((2, ROWS, 128), F32),
         v((2, ROWS, 128), F32),
         v((2, ROWS, 128), F32),
-        v((4, ROWS, 512), F32),
+        v((ROWS, 512), F32),
         v((3, ROWS, 512), BF16),
         v((3, ROWS, 512), BF16),
         v((2, 3, ROWS, COLS), BF16),
@@ -644,10 +549,8 @@
         v((ROWS, FFB), BF16),
         dma((6,)), dma((9,)), dma((9,)), dma((5,)), dma((3,)), dma((9,)),
         *gather_sems,
-        dma((16,)), dma((16,)), dma((3,)), dma((4, 3)), dma((16,)),
-        dma((2, 2)),
-        dma((2, 3)), dma((2, 3)), dma((2, 3)), dma((2, 3)), dma((2, 2, 3)), dma((2, 2, 3)),
-        dma((2, 2)), dma((2,)), dma((2, 2)),
+        dma((4, 3)), dma((4, 3)), dma((4, 3)), dma((4, 3)), dma((2, 2, 3)), dma((2, 2, 3)),
+        dma((2, 4)), dma((2, 2)),
     ]
     return pl.pallas_call(
         kernel,

time: 123 us -> 115 us (0.935)
  the two profiles are of different devices: /device:TPU:56 before, /device:TPU:34 now
where the time goes in v4:
time: 115 us
  Pallas kernels  114 us (99%)
  local copies, waits for them, and re-layouts  1.57 us (1%)
    pallas_call x1, Pallas kernels, shards(): pl.pallas_call(kernel, out_shape=jax.ShapeDtypeStruct((ROWS, COLS), BF16)...  114 us

profile of v4, /device:TPU:34, one launch (start us, length us, event | category | flops | bytes accessed | tf_op | source)
XLA Modules:
  0.0 115.3 jit_solution(9193460374004995760)
XLA Ops:
  0.0 113.7 %layer.1 = bf16[256,256]{1,0:T(8,128)(2,1)} custom-call(bf16[256,256]{1,0:T(8,128)(2,1)} %q_ref.1, bf16[256,256]{1,0:T(8,128)(2,1)} %res_ref.1, f32[2,32]{1,0:T(2,128)} %tab_ref.1, s32[2,33]{1,0:T(2,128)} %bk_ref.1, f32[1,2048]{1,0:T(1,128)} %bitcast.1, bf16[256,256]{1,0:T(8,128)(2,1)} %k_hbm.1, bf16[256,256]{1,0:T(8,128)(2,1)} %v_hbm.1, ...), custom_call_target="tpu_custom_call" | custom-call | tf_op jit(solution)/shard_map/layer/pallas_call | solution.py:555
  113.7 1.6 %copy.13 = bf16[256,256]{1,0:T(8,128)(2,1)} copy(bf16[256,256]{1,0:T(8,128)(2,1)} %layer.1) | data formatting | bytes 262144

commit v5 on v4

--- a/solution.py
+++ b/solution.py
@@ -312,8 +312,6 @@
     pl.when(across[1])(across[0].start)
     kv_sib(near[0]).start()
     second.append(across)
-    gw.zstep(1)
-    gw.ysend(0)
     for o, core in ((-4, 0), (-4, 1), (4, 0), (4, 1)):
         need = inside(o)
         if (o, core) == (-4, 0):
@@ -333,14 +331,21 @@
             for near_o in near[1:]:
                 got_own(near_o)
                 kv_sib(near_o).start()
-            gw.zstep(2)
-
-    gw.ysend(1)
+            gw.zstep(1)
+            gw.ysend(0)
+
     for n, o in enumerate(near):
         got_sib(o)
         attend(o)
-        gw.zstep(3 + n)
-        gw.ysend(2 + n)
+        if n == 0:
+            gw.zstep(2)
+            gw.ysend(1)
+        if n == 1:
+            gw.zstep(3)
+            gw.ysend(2)
+        if n == 2:
+            gw.zstep(4)
+            gw.ysend(3)
     for o in last:
 
         @pl.when(inside(o))
@@ -348,8 +353,8 @@
             got_own(o)
             kv_sib(o).start()
 
-    gw.zstep(6)
-    gw.ysend(5)
+    gw.zstep(5)
+    gw.ysend(4)
     for n, o in enumerate(last):
 
         @pl.when(inside(o))
@@ -358,9 +363,8 @@
             attend(o)
 
         if n == 0:
-            gw.zstep(7)
-            gw.ysend(6)
-            gw.ysend(7)
+            gw.zstep(6)
+            gw.ysend(5)
 
     for hd in (0, 1):
         att_own[:, 128 * hd : 128 * hd + 128] = (acc_ref[hd] / l_ref[hd]).astype(BF16)
@@ -392,6 +396,9 @@
         for d in (2, 1, 3):
             rs[2 * j + 1][d - 1].start()
 
+    gw.zstep(7)
+    gw.ysend(6)
+    gw.ysend(7)
     cross_a = [remote(mid_s.at[q], mid_r.at[q], ca.at[0, j], ca.at[1, j], at.far) for j, q in enumerate(quart)]
     for j, q in enumerate(quart):
         for d in rs[j]:

time: 115 us -> 112 us (0.974)
  the two profiles are of different devices: /device:TPU:34 before, /device:TPU:48 now
where the time goes in v5:
time: 112 us
  Pallas kernels  111 us (99%)
  local copies, waits for them, and re-layouts  1.57 us (1%)
    pallas_call x1, Pallas kernels, shards(): pl.pallas_call(kernel, out_shape=jax.ShapeDtypeStruct((ROWS, COLS), BF16)...  111 us

profile of v5, /device:TPU:48, one launch (start us, length us, event | category | flops | bytes accessed | tf_op | source)
XLA Modules:
  0.0 112.1 jit_solution(8869974430262288134)
XLA Ops:
  0.0 110.5 %layer.1 = bf16[256,256]{1,0:T(8,128)(2,1)} custom-call(bf16[256,256]{1,0:T(8,128)(2,1)} %q_ref.1, bf16[256,256]{1,0:T(8,128)(2,1)} %res_ref.1, f32[2,32]{1,0:T(2,128)} %tab_ref.1, s32[2,33]{1,0:T(2,128)} %bk_ref.1, f32[1,2048]{1,0:T(1,128)} %bitcast.1, bf16[256,256]{1,0:T(8,128)(2,1)} %k_hbm.1, bf16[256,256]{1,0:T(8,128)(2,1)} %v_hbm.1, ...), custom_call_target="tpu_custom_call" | custom-call | tf_op jit(solution)/shard_map/layer/pallas_call | solution.py:562
  110.5 1.6 %copy.13 = bf16[256,256]{1,0:T(8,128)(2,1)} copy(bf16[256,256]{1,0:T(8,128)(2,1)} %layer.1) | data formatting | bytes 262144
